TPU v7x, 512 devices: a whole 4x8x8 slice. The times are simulated.
512 devices in a mesh: shot: 16 (over y, core), brick: 32 (over x, z).
Axes of the slice: x: 4, y: 8, z: 8, core: 2. Of those that a mesh axis runs over, the one named last changes fastest.
Arguments:
- pressure: float32 [128, 1024, 512], P('shot', 'brick'), may hold values from -6 to 6
- auxiliary: float32 [128, 1024, 512], P('shot', 'brick'), may hold values from -6 to 6
- pressure_prior: float32 [128, 1024, 512], P('shot', 'brick'), may hold values from -6 to 6
- auxiliary_prior: float32 [128, 1024, 512], P('shot', 'brick'), may hold values from -6 to 6
- courant_sq: float32 [1024, 512], P('brick'), may hold values from 0.05 to 0.2
- thomsen_epsilon: float32 [1024, 512], P('brick'), may hold values from 0.1 to 0.35
- thomsen_delta: float32 [1024, 512], P('brick'), may hold values from 0 to 0.1
- tilt_angle: float32 [1024, 512], P('brick'), may hold values from -3.140625 to 3.140625
- frequencies: float32 [16], replicated, may hold values from 0.05 to 1.5
- spectra: float32 [128, 32, 16384], P('shot', None, 'brick'), may hold values from -6 to 6
- target_cells: int32 [16384], P('brick'), may hold values from 0 to 16383, as said below
- patch_lists: int32 [32, 16, 3, 128], P('brick'), may hold values from 0 to 511, as said below
- patch_counts: int32 [32, 16], P('brick', 'shot'), may hold values from 1 to 3, as said below
Outputs:
- pressure_out: float32 [128, 1024, 512], P('shot', 'brick')
- auxiliary_out: float32 [128, 1024, 512], P('shot', 'brick')
- spectra_out: float32 [128, 32, 16384], P('shot', None, 'brick')
- gram_tiles: float32 [32, 16, 3, 128, 128], P('brick', 'shot')
Inputs may be any that keep to these rules, and one draw needn't show every extreme that they name: `target_cells`: the block of each brick holds distinct cells of that brick. `patch_lists`: target numbers within the owner's brick; the cells of one patch slot are distinct. `patch_counts`: in every brick some owner has all 3 slots live.
All inputs are finite; a program needn't handle non-finite values.
Results may differ from a plain program's by a relative error of at most 0.00077.
Values may be sent and summed in bfloat16 or wider, within the bound.
A program may use at most 64 MiB of HBM per device.

v0:
```python
import jax
import jax.numpy as jnp
from jax import lax
from jax.sharding import PartitionSpec as P

STEPS = 4
PATCH = 128
P_MAX = 3


def with_halo(cells, sides, width):
    for axis, dim in sides:
        count = lax.axis_size(axis)
        ends = count - 1
        head = lax.slice_in_dim(cells, 0, width, axis=dim)
        tail = lax.slice_in_dim(cells, cells.shape[dim] - width, cells.shape[dim], axis=dim)
        cells = jnp.concatenate(
            [
                lax.ppermute(tail, axis, [(i, (i + 1) % count) for i in range(ends)]),
                cells,
                lax.ppermute(head, axis, [((i + 1) % count, i) for i in range(ends)]),
            ],
            axis=dim,
        )
    return cells


def tilt_terms(tilt_angle):
    sine = jnp.sin(tilt_angle)
    cosine = jnp.cos(tilt_angle)
    return (sine * sine, cosine * cosine, 2.0 * sine * cosine)


def derivatives(field, sine_sq, cosine_sq, double_sin):
    widths = [(0, 0)] * (field.ndim - 1) + [(1, 1)]
    padded = jnp.pad(field, widths)
    centre = padded[..., 1:-1, 1:-1]
    second_x = padded[..., 2:, 1:-1] - 2.0 * centre + padded[..., :-2, 1:-1]
    second_z = padded[..., 1:-1, 2:] - 2.0 * centre + padded[..., 1:-1, :-2]
    mixed = 0.25 * (
        padded[..., 2:, 2:] - padded[..., 2:, :-2] - padded[..., :-2, 2:] + padded[..., :-2, :-2]
    )
    along_axis = sine_sq * second_x + cosine_sq * second_z + double_sin * mixed
    across_axis = second_x + second_z - along_axis
    return (along_axis, across_axis)


def leapfrog(extended, former, coefficients):
    courant_sq, epsilon, delta_value, sine_sq, cosine_sq, double_sin = coefficients
    along_p, across_p = derivatives(extended[0], sine_sq, cosine_sq, double_sin)
    along_q, across_q = derivatives(extended[1], sine_sq, cosine_sq, double_sin)
    pressure = extended[0][..., 1:-1, :]
    auxiliary = extended[1][..., 1:-1, :]
    pressure_next = (
        2.0 * pressure - former[0] + courant_sq * ((1.0 + 2.0 * epsilon) * across_p + along_q)
    )
    auxiliary_next = (
        2.0 * auxiliary - former[1] + courant_sq * ((1.0 + 2.0 * delta_value) * across_p + along_q)
    )
    return jnp.stack([pressure_next, auxiliary_next])


def shards(
    pressure,
    auxiliary,
    pressure_prior,
    auxiliary_prior,
    courant_sq,
    thomsen_epsilon,
    thomsen_delta,
    tilt_angle,
    frequencies,
    spectra,
    target_cells,
    patch_lists,
    patch_counts,
):
    shots_here, width_x, depth = pressure.shape
    samples = []
    packed = jnp.concatenate(
        [
            jnp.stack([pressure, auxiliary, pressure_prior, auxiliary_prior]).reshape(
                4 * shots_here, width_x, depth
            ),
            jnp.stack([courant_sq, thomsen_epsilon, thomsen_delta, tilt_angle]),
        ],
        0,
    )
    widened = with_halo(packed, (("brick", 1),), STEPS)
    states = widened[: 4 * shots_here].reshape(4, shots_here, width_x + 2 * STEPS, depth)
    params = widened[4 * shots_here :]
    sine_sq, cosine_sq, double_sin = tilt_terms(params[3])
    full_coefficients = (params[0], params[1], params[2], sine_sq, cosine_sq, double_sin)
    current = states[:2]
    former = states[2:]
    for moment in range(STEPS):
        trimmed = moment + 1
        coefficients = tuple(
            (item[trimmed : item.shape[0] - trimmed] for item in full_coefficients)
        )
        advanced = leapfrog(current, former[:, :, 1:-1], coefficients)
        former = current[:, :, 1:-1]
        current = advanced
        margin = STEPS - moment - 1
        interior = current[0][:, margin : margin + width_x]
        samples.append(
            jnp.take(interior.reshape(shots_here, width_x * depth), target_cells, axis=1)
        )
    spectra_out = spectra
    for moment in range(STEPS):
        angle = frequencies * (moment + 1.0)
        table = jnp.concatenate([jnp.cos(angle), -jnp.sin(angle)])
        spectra_out = spectra_out + table[None, :, None] * samples[moment][:, None, :]
    local_features = spectra_out.shape[0] * spectra_out.shape[1]
    features = spectra_out.reshape(local_features, spectra_out.shape[2]).astype(jnp.bfloat16)
    owners = patch_lists.shape[1]
    total_features = local_features * owners
    live_slots = (jnp.arange(P_MAX, dtype=jnp.int32) < patch_counts[0, 0]).astype(jnp.float32)
    own_lists = lax.dynamic_index_in_dim(
        patch_lists[0], lax.axis_index("shot"), 0, keepdims=False
    ).reshape(-1)
    portion = lax.all_gather(features, "shot", axis=0, tiled=True)
    selected = jnp.take(portion, own_lists, axis=1).reshape(portion.shape[0], P_MAX, PATCH)
    grams = jnp.einsum("fpa,fpb->pab", selected, selected, preferred_element_type=jnp.float32)
    gram_tiles = grams / total_features * live_slots[:, None, None]
    return (current[0], current[1], spectra_out, gram_tiles.reshape(1, 1, P_MAX, PATCH, PATCH))


def solution(mesh):
    return jax.shard_map(
        shards,
        mesh=mesh,
        in_specs=(
            P("shot", "brick", None),
            P("shot", "brick", None),
            P("shot", "brick", None),
            P("shot", "brick", None),
            P("brick", None),
            P("brick", None),
            P("brick", None),
            P("brick", None),
            P(),
            P("shot", None, "brick"),
            P("brick"),
            P("brick", None, None, None),
            P("brick", "shot"),
        ),
        out_specs=(
            P("shot", "brick", None),
            P("shot", "brick", None),
            P("shot", None, "brick"),
            P("brick", "shot", None, None, None),
        ),
        check_vma=False,
    )
```

profile of v0, /device:TPU:7, one launch (start us, length us, event | category | flops | bytes accessed | tf_op | source)
XLA Modules:
  0.0 155.4 jit_solution(15979312028043918637)
XLA Ops:
  7.2 0.0 all-gather.2.cloned.1.call-start
  7.2 1.7 %pad_maximum_fusion.1 = f32[4,8,32,512]{3,2,1,0:T(8,128)S(1)} fusion(f32[1,8,32,512]{3,2,1,0:T(8,128)} %bitcast.150, f32[1,8,32,512]{3,2,1,0:T(8,128)} %bitcast.151, f32[1,8,32,512]{3,2,1,0:T(8,128)} %bitcast.152, f32[1,8,32,512]{3,2,1,0:T(8,128)} %bitcast.153), kind=kLoop, calls=%fused_computation.9 | loop fusion | flops 1572864 | bytes 4194304 | tf_op jit(solution)/shard_map/stack | solution.py:82
  8.9 0.0 copy-start.1
  8.9 0.0 copy-start.3
  8.9 0.0 copy-start.4
  9.0 0.0 copy-start.5
  9.0 0.0 copy-start.6
  9.0 0.0 copy-start.7
  9.0 0.2 constant_dynamic-update-slice_fusion
  9.2 0.6 copy-done.1
  9.8 0.0 copy-done.3
  9.8 0.0 copy-done.4
  9.8 0.0 copy-done.5
  9.9 0.1 fusion.128
  10.0 4.0 %collective-permute-start = (f32[36,4,512]{2,1,0:T(4,128)S(1)}, f32[36,4,512]{2,1,0:T(4,128)S(1)}, u32[]{:S(2)}, u32[]{:S(2)}) collective-permute-start(f32[36,4,512]{2,1,0:T(4,128)S(1)} %get-tuple-element.36), channel_id=1, source_target_pairs={{0,1},{1,2},{2,3},{3,4},{4,5},{5,6},{6,7},{7,8},{8,9},{9,10},{10,1... | collective-permute-start | bytes 884744 | tf_op jit(solution)/shard_map/ppermute | solution.py:19
  14.0 8.9 %collective-permute-start.1 = (f32[36,4,512]{2,1,0:T(4,128)S(1)}, f32[36,4,512]{2,1,0:T(4,128)S(1)}, u32[]{:S(2)}, u32[]{:S(2)}) collective-permute-start(f32[36,4,512]{2,1,0:T(4,128)S(1)} %get-tuple-element.37), channel_id=1, source_target_pairs={{1,0},{2,1},{3,2},{4,3},{5,4},{6,5},{7,6},{8,7},{9,8},{10,9},{11,1... | collective-permute-start | bytes 884744 | tf_op jit(solution)/shard_map/ppermute | solution.py:21
  22.9 0.0 copy-done.6
  22.9 0.0 copy-done.7
  22.9 0.1 fusion.130
  23.0 0.1 pad_maximum_fusion.3
  23.1 0.1 pad_maximum_fusion.5
  23.2 4.4 %collective-permute-done = f32[36,4,512]{2,1,0:T(4,128)S(1)} collective-permute-done((f32[36,4,512]{2,1,0:T(4,128)S(1)}, f32[36,4,512]{2,1,0:T(4,128)S(1)}, u32[]{:S(2)}, u32[]{:S(2)}) %collective-permute-start) | collective-permute-done | bytes 294944 | tf_op jit(solution)/shard_map/ppermute | solution.py:19
  27.6 0.9 collective-permute-done.1
  28.5 0.3 fusion.125
  28.8 0.3 multiply_multiply_fusion
  29.2 0.4 pad_maximum_fusion
  29.7 0.1 fusion.126
  29.8 0.3 fusion.127
  30.1 0.1 fusion.106
  30.1 2.3 %fusion.75 = (f32[8,38,512]{2,1,0:T(8,128)S(1)}, f32[8,38,512]{2,1,0:T(8,128)S(1)}, f32[8,38,512]{2,1,0:T(8,128)S(1)}) fusion(f32[2,8,40,512]{3,2,1,0:T(8,128)S(1)} %bitcast.146, f32[36,40,512]{2,1,0:T(8,128)S(1)} %pad_maximum_fusion, f32[38,512]{1,0:T(8,128)S(1)} %get-tuple-element.30, f32[38,512]{1,0:T(8,128)S(1)} %get-tuple-element.31, ...), kind=kLoop, calls=%fused_computation.149 | loop fusion | flops 5136384 | bytes 7925760 | tf_op jit(solution)/shard_map/add | solution.py:55
  32.4 0.1 slice.654
  32.5 0.3 fusion.70
  32.8 0.1 fusion.109
  32.9 2.3 %fusion.65 = (f32[8,36,512]{2,1,0:T(8,128)S(1)}, f32[8,36,512]{2,1,0:T(8,128)S(1)}, f32[8,36,512]{2,1,0:T(8,128)S(1)}) fusion(f32[2,8,40,512]{3,2,1,0:T(8,128)S(1)} %bitcast.144, f32[8,38,512]{2,1,0:T(8,128)S(1)} %fusion.70, f32[36,512]{1,0:T(8,128)S(1)} %get-tuple-element.27, f32[36,512]{1,0:T(8,128)S(1)} %get-tuple-element.28, ...), kind=kLoop, calls=%fused_computation.121 | loop fusion | flops 4866048 | bytes 8077312 | tf_op jit(solution)/shard_map/add | solution.py:58
  35.2 0.3 fusion.72
  35.5 0.1 slice.655
  35.6 0.1 fusion.99
  35.6 2.3 %fusion.67 = (f32[8,34,512]{2,1,0:T(8,128)S(1)}, f32[8,34,512]{2,1,0:T(8,128)S(1)}, f32[8,34,512]{2,1,0:T(8,128)S(1)}) fusion(f32[1,8,38,512]{3,2,1,0:T(8,128)S(1)} %bitcast.135, f32[8,36,512]{2,1,0:T(8,128)S(1)} %fusion.72, f32[34,512]{1,0:T(8,128)S(1)} %get-tuple-element.24, f32[34,512]{1,0:T(8,128)S(1)} %get-tuple-element.25, ...), kind=kLoop, calls=%fused_computation.126 | loop fusion | flops 4595712 | bytes 7979008 | tf_op jit(solution)/shard_map/add | solution.py:55
  37.9 0.3 fusion.62
  38.3 2.6 %fusion.94 = (f32[8,32,512]{2,1,0:T(8,128)}, f32[8,32,512]{2,1,0:T(8,128)S(1)}, f32[8,32,512]{2,1,0:T(8,128)S(1)}) fusion(f32[1,8,36,512]{3,2,1,0:T(8,128)S(1)} %bitcast.136, f32[8,34,512]{2,1,0:T(8,128)S(1)} %fusion.62, f32[32,512]{1,0:T(8,128)S(1)} %multiply_add_fusion.1, f32[32,512]{1,0:T(8,128)S(1)} %copy-done.1, f32[32,512]{1,0:T(8,128)S(1)} %get-tuple-element.61, ...), kind=kLoop, calls=%fused_computation.170 | loop fusion | flops 4325376 | bytes 6881280 | tf_op jit(solution)/shard_map/add | solution.py:58
  40.8 0.5 fusion.129
  41.3 0.0 copy-start
  41.3 4.6 %copy.31 = f32[8,32,512]{0,2,1:T(8,128)} copy(f32[8,32,512]{2,1,0:T(8,128)S(1)} %get-tuple-element.38) | data formatting | bytes 1048576 | tf_op jit(solution)/shard_map/slice | solution.py:52
  46.0 4.7 %copy.29 = f32[8,32,512]{0,2,1:T(8,128)} copy(f32[8,32,512]{2,1,0:T(8,128)S(1)} %slice.655) | data formatting | bytes 1048576 | tf_op jit(solution)/shard_map/slice | solution.py:105
  50.6 4.4 %gather_fusion.3 = f32[512,8]{1,0:T(8,128)S(1)} fusion(f32[8,16384]{0,1:T(8,128)} %bitcast.139, s32[1024]{0:T(1024)S(1)} %pad_clamp_fusion.1), kind=kCustom, calls=%fused_computation.2.clone | custom fusion | bytes 34816 | tf_op jit(solution)/shard_map/jit(_take)/gather | solution.py:107
  55.0 4.4 %gather_fusion.2 = f32[512,8]{1,0:T(8,128)S(1)} fusion(f32[8,16384]{0,1:T(8,128)} %bitcast.140, s32[1024]{0:T(1024)S(1)} %pad_clamp_fusion.1), kind=kCustom, calls=%fused_computation.1.clone | custom fusion | bytes 34816 | tf_op jit(solution)/shard_map/jit(_take)/gather | solution.py:107
  59.4 4.7 %copy.27 = f32[8,32,512]{0,2,1:T(8,128)} copy(f32[8,32,512]{2,1,0:T(8,128)S(1)} %slice.654) | data formatting | bytes 1048576 | tf_op jit(solution)/shard_map/slice | solution.py:105
  64.1 4.4 %gather_fusion.1 = f32[512,8]{1,0:T(8,128)S(1)} fusion(f32[8,16384]{0,1:T(8,128)} %bitcast.141, s32[1024]{0:T(1024)S(1)} %pad_clamp_fusion.1), kind=kCustom, calls=%fused_computation.clone | custom fusion | bytes 34816 | tf_op jit(solution)/shard_map/jit(_take)/gather | solution.py:107
  68.5 0.0 copy-done
  68.5 4.7 %copy.33 = f32[8,32,512]{0,2,1:T(8,128)} copy(f32[8,32,512]{2,1,0:T(8,128)S(1)} %get-tuple-element.39) | data formatting | bytes 1048576 | tf_op jit(solution)/shard_map/add | solution.py:55
  73.2 4.5 %gather_fusion.4 = f32[512,8]{1,0:T(8,128)S(1)} fusion(f32[8,16384]{0,1:T(8,128)} %bitcast.142, s32[1024]{0:T(1024)S(1)} %pad_clamp_fusion.1), kind=kCustom, calls=%fused_computation.3.clone | custom fusion | bytes 34816 | tf_op jit(solution)/shard_map/jit(_take)/gather | solution.py:107
  77.7 0.1 select_bitcast_fusion.3
  77.8 0.1 copy.28
  77.9 0.1 copy.30
  78.0 0.1 copy.32
  78.1 0.1 copy.34
  78.2 0.0 copy-done.2
  78.2 1.0 fusion.116
  79.3 0.8 copy.35
  80.1 0.0 all-gather.2.cloned.1.call-update
  80.8 0.7 fusion.114
  81.5 51.4 %all-gather.2.cloned.1.call-done = bf16[4096,512]{0,1:T(8,128)(2,1)} async-done(((bf16[256,512]{0,1:T(8,128)(2,1)}), bf16[4096,512]{0,1:T(8,128)(2,1)}) %all-gather.2.cloned.1.call-update) | async-done | bytes 4194320 | tf_op jit(solution)/shard_map/all_gather | solution.py:122
  133.0 10.9 %gather_fusion = bf16[384,4096]{1,0:T(8,128)(2,1)} fusion(bf16[4096,512]{0,1:T(8,128)(2,1)} %all-gather.2.cloned.1.call-done, s32[1024]{0:T(1024)S(1)} %pad_clamp_fusion), kind=kCustom, calls=%fused_computation.4 | custom fusion | bytes 6292992 | tf_op jit(solution)/shard_map/jit(_take)/gather | solution.py:123
  143.9 4.6 %fusion.7 = f32[1,1,3,128,128]{4,3,2,1,0:T(8,128)} fusion(bf16[4096,3,128]{0,2,1:T(8,128)(2,1)} %bitcast.148, pred[3,128]{1,0:T(4,128)(4,1)S(1)} %compare_and_fusion.1, f32[3]{0:T(128)S(1)} %compare_select_fusion.3), kind=kOutput, calls=%fused_computation.12 | convolution fusion | flops 404275200 | bytes 3342732 | tf_op jit(solution)/shard_map/fpa,fpb->pab/dot_general | solution.py:124
  (18 shorter events, 0.2 us)
Async XLA Ops:
  7.2 125.8 %all-gather.2.cloned.1.call-start = ((), (), s32[]{:S(2)}) async-start(), calls=%async_computation | async-start | bytes 4456448 | tf_op jit(solution)/shard_map/all_gather | solution.py:122
  8.9 0.8 copy-start.1
  8.9 0.9 copy-start.3
  8.9 0.9 copy-start.4
  9.0 0.9 copy-start.5
  9.0 13.9 %copy-start.6 = (s32[512]{0:T(512)S(1)}, s32[512]{0:T(512)}, u32[]{:S(2)}) copy-start(s32[512]{0:T(512)} %param.25) | copy-start | bytes 6148
  9.0 14.0 %copy-start.7 = (f32[16]{0:T(128)S(1)}, f32[16]{0:T(128)}, u32[]{:S(2)}) copy-start(f32[16]{0:T(128)} %param.23) | copy-start | bytes 196
  10.0 17.6 %collective-permute-start = (f32[36,4,512]{2,1,0:T(4,128)S(1)}, f32[36,4,512]{2,1,0:T(4,128)S(1)}, u32[]{:S(2)}, u32[]{:S(2)}) collective-permute-start(f32[36,4,512]{2,1,0:T(4,128)S(1)} %get-tuple-element.36), channel_id=1, source_target_pairs={{0,1},{1,2},{2,3},{3,4},{4,5},{5,6},{6,7},{7,8},{8,9},{9,10},{10,1... | collective-permute-start | bytes 884744 | tf_op jit(solution)/shard_map/ppermute | solution.py:19
  14.0 14.5 %collective-permute-start.1 = (f32[36,4,512]{2,1,0:T(4,128)S(1)}, f32[36,4,512]{2,1,0:T(4,128)S(1)}, u32[]{:S(2)}, u32[]{:S(2)}) collective-permute-start(f32[36,4,512]{2,1,0:T(4,128)S(1)} %get-tuple-element.37), channel_id=1, source_target_pairs={{1,0},{2,1},{3,2},{4,3},{5,4},{6,5},{7,6},{8,7},{9,8},{10,9},{11,1... | collective-permute-start | bytes 884744 | tf_op jit(solution)/shard_map/ppermute | solution.py:21
  41.3 27.2 %copy-start = (f32[8,32,512]{2,1,0:T(8,128)}, f32[8,32,512]{2,1,0:T(8,128)S(1)}, u32[]{:S(2)}) copy-start(f32[8,32,512]{2,1,0:T(8,128)S(1)} %get-tuple-element.39) | copy-start | bytes 1572868
  73.2 5.0 %copy-start.2 = (f32[8,32,512]{2,1,0:T(8,128)S(1)}, f32[8,32,512]{2,1,0:T(8,128)}, u32[]{:S(2)}) copy-start(f32[8,32,512]{2,1,0:T(8,128)} %param.24) | copy-start | bytes 1572868
Sparse Core Ops, SparseCore 0:
  80.2 52.6 all-gather.1
where the time goes:
time: 158 us; the launch traced here: 155 us
  waiting for transfers between devices  56.8 us (36%)
  local copies, waits for them, and re-layouts  50 us (32%)
  other arithmetic  16 us (10%)
  between operations  15.1 us (10%)
  starting transfers between devices  12.9 us (8%)
  matrix products  4.63 us (3%)
    all_gather x1, waiting for transfers between devices, shards(): portion = lax.all_gather(features, 'shot', axis=0, tiled=True)  51.4 us
    gather x4, local copies, waits for them, and re-layouts, shards(): jnp.take(interior.reshape(shots_here, width_x * depth), target_cells, axi...  17.7 us
    gather x1, local copies, waits for them, and re-layouts, shards(): jnp.take(portion, own_lists, axis=1).reshape(portion.shape[0], P_MAX, PATCH)  10.9 us
    slice x4, local copies, waits for them, and re-layouts, shards(): interior = current[0][:, margin:margin + width_x]  9.44 us
    ppermute x1, starting transfers between devices, with_halo(): lax.ppermute(head, axis, [((i + 1) % count, i) for i in range(ends)])  8.85 us
    add x4, other arithmetic, leapfrog(): 2.0 * auxiliary - former[1]  5.53 us
    add x3, other arithmetic, leapfrog(): 2.0 * pressure - former[0]  4.87 us
    add x1, local copies, waits for them, and re-layouts, leapfrog(): 2.0 * pressure - former[0]  4.66 us
  transfers between devices with their start and end apart: 3, of which 3 were waited for; matrix products, arithmetic and copies ran while one was open for 1% of the time, Pallas kernels for 0%

commit v1 on v0

v1 whole, which is shorter than its diff:
```python
import functools

import jax
import jax.numpy as jnp
from jax import lax
from jax.experimental import pallas as pl
from jax.experimental.pallas import tpu as pltpu
from jax.sharding import PartitionSpec as P

STEPS = 4
PATCH = 128
P_MAX = 3
SHOTS = 8
ROWS = 32
HALO = 4
DEPTH = 512
TILES = DEPTH // 128
CHIPS = 8
CHUNK = 80
MESH = pl.DeviceIdType.MESH
F32 = jnp.float32
BF16 = jnp.bfloat16

FAR_FIRST = (4, 3, 5, 2, 6, 1, 7)
NEAR_FIRST = (1, 7, 2, 6, 3, 5, 4)


def split(value):
    high = value.astype(BF16)
    return high, (value - high.astype(F32)).astype(BF16)


def kernel(
    bricks,
    freq_ref,
    counts_ref,
    courant_ref,
    epsilon_ref,
    delta_ref,
    tilt_ref,
    cells_ref,
    lists_ref,
    p_in,
    q_in,
    pp_in,
    qq_in,
    spectra_in,
    p_out,
    q_out,
    spectra_out,
    gram_ref,
    pbuf,
    qbuf,
    coef,
    slab_out,
    slab_in,
    rim_out,
    rim_in,
    spec,
    onehot,
    samples,
    feats,
    half,
    part_in,
    gathered,
    in_sem,
    out_sem,
    halo_send,
    halo_recv,
    feat_send,
    feat_recv,
    part_send,
    part_recv,
    ring_send,
    ring_recv,
    pass_send,
    pass_recv,
):
    shot = lax.axis_index("shot")
    brick = lax.axis_index("brick")
    chip = shot // 2
    core = lax.rem(shot, 2)
    has_left = brick > 0
    has_right = brick < bricks - 1

    barrier = pltpu.get_barrier_semaphore()
    for other in range(1, 2 * CHIPS):
        pl.semaphore_signal(
            barrier,
            inc=1,
            device_id={"shot": lax.rem(shot + other, 2 * CHIPS)},
            device_id_type=MESH,
        )

    @pl.when(has_left)
    def _():
        pl.semaphore_signal(barrier, inc=1, device_id={"brick": brick - 1}, device_id_type=MESH)

    @pl.when(has_right)
    def _():
        pl.semaphore_signal(barrier, inc=1, device_id={"brick": brick + 1}, device_id_type=MESH)

    loads = []
    for number, (source, target, slot) in enumerate(
        ((p_in, pbuf, 1), (q_in, qbuf, 1), (pp_in, pbuf, 0), (qq_in, qbuf, 0))
    ):
        for s in range(SHOTS):
            loads.append(
                pltpu.make_async_copy(
                    source.at[s],
                    target.at[slot, pl.ds(HALO, ROWS), s],
                    in_sem.at[number],
                )
            )
    for load in loads:
        load.start()
    spectra_load = pltpu.make_async_copy(spectra_in, spec, in_sem.at[4])
    spectra_load.start()

    sine = jnp.sin(tilt_ref[...])
    cosine = jnp.cos(tilt_ref[...])
    courant = courant_ref[...]
    own = pl.ds(8, ROWS)
    coef[0, own] = cosine * cosine
    coef[1, own] = 0.5 * sine * cosine
    coef[2, own] = courant
    coef[3, own] = courant * (1.0 + 2.0 * epsilon_ref[...])
    coef[4, own] = courant * (1.0 + 2.0 * delta_ref[...])
    for number in range(5):
        rim_out[0, pl.ds(3 * number, 3)] = coef[number, pl.ds(8, 3)]
        rim_out[1, pl.ds(3 * number, 3)] = coef[number, pl.ds(8 + ROWS - 3, 3)]
    rim_out[0, pl.ds(15, 1)] = jnp.zeros((1, DEPTH), F32)
    rim_out[1, pl.ds(15, 1)] = jnp.zeros((1, DEPTH), F32)

    for load in loads:
        load.wait()
    for side in range(2):
        first = HALO if side == 0 else HALO + ROWS - 4
        for row in range(4):
            slab_out[side, row] = jnp.concatenate(
                [pbuf[1, first + row], qbuf[1, first + row]], axis=0
            ).astype(BF16)
        first = HALO if side == 0 else HALO + ROWS - 3
        for row in range(3):
            slab_out[side, 4 + row] = jnp.concatenate(
                [pbuf[0, first + row], qbuf[0, first + row]], axis=0
            ).astype(BF16)

    pl.semaphore_wait(
        barrier, 2 * CHIPS - 1 + has_left.astype(jnp.int32) + has_right.astype(jnp.int32)
    )

    def halo_copies(side):
        target = {"brick": brick - 1 if side == 0 else brick + 1}
        return [
            pltpu.make_async_remote_copy(
                src_ref=slab_out.at[side],
                dst_ref=slab_in.at[1 - side],
                send_sem=halo_send.at[side, 0],
                recv_sem=halo_recv.at[1 - side, 0],
                device_id=target,
                device_id_type=MESH,
            ),
            pltpu.make_async_remote_copy(
                src_ref=rim_out.at[side],
                dst_ref=rim_in.at[1 - side],
                send_sem=halo_send.at[side, 1],
                recv_sem=halo_recv.at[1 - side, 1],
                device_id=target,
                device_id_type=MESH,
            ),
        ]

    for side, there in ((0, has_left), (1, has_right)):

        @pl.when(there)
        def _():
            for copy in halo_copies(side):
                copy.start()

    lane = lax.broadcasted_iota(jnp.int32, (SHOTS, 128), 1)
    first_lane = lane == 0
    last_lane = lane == 127

    def tiles(value):
        return [value[:, 128 * k : 128 * (k + 1)] for k in range(TILES)]

    def deeper(value):
        turned = [pltpu.roll(tile, 127, 1) for tile in value]
        turned.append(jnp.zeros((SHOTS, 128), F32))
        return [jnp.where(last_lane, turned[k + 1], turned[k]) for k in range(TILES)]

    def shallower(value):
        turned = [jnp.zeros((SHOTS, 128), F32)] + [pltpu.roll(tile, 1, 1) for tile in value]
        return [jnp.where(first_lane, turned[k], turned[k + 1]) for k in range(TILES)]

    def stencil(above, here, below):
        steep = [b + a for a, b in zip(above, below)]
        slope = [b - a for a, b in zip(above, below)]
        deep = [a + b for a, b in zip(deeper(here), shallower(here))]
        cross = [a - b for a, b in zip(deeper(slope), shallower(slope))]
        return steep, deep, cross

    def two_rows(moment, row):
        p_rows = [tiles(pbuf[moment, row + k]) for k in range(-1, 3)]
        q_rows = [tiles(qbuf[moment, row + k]) for k in range(-1, 3)]
        for k in range(2):
            at = row + k
            cos_sq, twist, speed, speed_e, speed_d = (
                tiles(jnp.broadcast_to(coef[number, pl.ds(at + 4, 1)], (SHOTS, DEPTH)))
                for number in range(5)
            )
            p_steep, p_deep, p_cross = stencil(p_rows[k], p_rows[k + 1], p_rows[k + 2])
            q_steep, q_deep, q_cross = stencil(q_rows[k], q_rows[k + 1], q_rows[k + 2])
            p_old = tiles(pbuf[moment - 1, at])
            q_old = tiles(qbuf[moment - 1, at])
            for t in range(TILES):
                p_two = p_rows[k + 1][t] + p_rows[k + 1][t]
                q_two = q_rows[k + 1][t] + q_rows[k + 1][t]
                sin_sq = 1.0 - cos_sq[t]
                across = cos_sq[t] * p_steep[t] + sin_sq * p_deep[t] - twist[t] * p_cross[t] - p_two
                along = sin_sq * q_steep[t] + cos_sq[t] * q_deep[t] + twist[t] * q_cross[t] - q_two
                push = speed[t] * along
                lanes = pl.ds(128 * t, 128)
                pbuf[moment + 1, at, :, lanes] = (p_two - p_old[t]) + (speed_e[t] * across + push)
                qbuf[moment + 1, at, :, lanes] = (q_two - q_old[t]) + (speed_d[t] * across + push)

    def inner_step(moment, carry):
        def pair(number, carry):
            two_rows(moment, moment + HALO + 2 * number)
            return carry

        return lax.fori_loop(0, ROWS // 2 - moment, pair, carry)

    lax.fori_loop(1, STEPS + 1, inner_step, 0)

    cells = cells_ref[...]
    target_x = cells >> 9
    target_z = cells & (DEPTH - 1)
    onehot[...] = (
        lax.broadcasted_iota(jnp.int32, (DEPTH, DEPTH), 0) == target_z
    ).astype(F32).astype(BF16)

    def picked(moment, first, count):
        rows = pbuf[moment + 1, pl.ds(first + HALO, count)].reshape(count * SHOTS, DEPTH)
        high, low = split(rows)
        values = jnp.dot(high, onehot[...], preferred_element_type=F32) + jnp.dot(
            low, onehot[...], preferred_element_type=F32
        )
        total = jnp.zeros((SHOTS, DEPTH), F32)
        for k in range(count):
            total = total + jnp.where(
                target_x == first + k, values[k * SHOTS : (k + 1) * SHOTS], 0.0
            )
        return total

    def inner_samples(moment, carry):
        samples[moment - 1] = picked(moment, HALO, ROWS - 2 * HALO)
        return carry

    lax.fori_loop(1, STEPS + 1, inner_samples, 0)

    number = lax.broadcasted_iota(jnp.int32, (16, 128), 0)
    frequency = jnp.zeros((16, 128), F32)
    for k in range(16):
        frequency = jnp.where(number == k, freq_ref[k], frequency)
    tables = []
    for moment in range(STEPS):
        angle = frequency * (moment + 1.0)
        tables.append(jnp.concatenate([jnp.cos(angle), -jnp.sin(angle)], axis=0))

    for side, there in ((0, has_left), (1, has_right)):

        @pl.when(there)
        def _():
            for copy in halo_copies(1 - side):
                copy.wait_recv()

        @pl.when(jnp.logical_not(there))
        def _():
            slab_in[side] = jnp.zeros((7, 16, DEPTH), BF16)
            rim_in[side] = jnp.zeros((16, DEPTH), F32)

    for side in range(2):
        first = 0 if side == 0 else HALO + ROWS
        for row in range(4):
            both = slab_in[side, row].astype(F32)
            pbuf[1, first + row] = both[:SHOTS]
            qbuf[1, first + row] = both[SHOTS:]
        first = 1 if side == 0 else HALO + ROWS
        for row in range(3):
            both = slab_in[side, 4 + row].astype(F32)
            pbuf[0, first + row] = both[:SHOTS]
            qbuf[0, first + row] = both[SHOTS:]
        for k in range(5):
            coef[k, pl.ds(first + 4, 3)] = rim_in[side, pl.ds(3 * k, 3)]

    def outer_step(moment, carry):
        def pair(number, carry):
            two_rows(
                moment,
                jnp.where(number < 2, moment + 2 * number, ROWS - moment + 2 * number),
            )
            return carry

        return lax.fori_loop(0, 4, pair, carry)

    lax.fori_loop(1, STEPS + 1, outer_step, 0)

    stores = []
    for number, (source, target) in enumerate(((pbuf, p_out), (qbuf, q_out))):
        for s in range(SHOTS):
            stores.append(
                pltpu.make_async_copy(
                    source.at[STEPS + 1, pl.ds(HALO, ROWS), s],
                    target.at[s],
                    out_sem.at[number],
                )
            )
    for store in stores:
        store.start()

    def outer_samples(moment, carry):
        samples[moment - 1] = (
            samples[moment - 1] + picked(moment, 0, HALO) + picked(moment, ROWS - HALO, HALO)
        )
        return carry

    lax.fori_loop(1, STEPS + 1, outer_samples, 0)

    spectra_load.wait()

    def transform(s, carry):
        drawn = [samples[moment, pl.ds(s, 1)] for moment in range(STEPS)]
        for t in range(TILES):
            lanes = pl.ds(128 * t, 128)
            value = spec[s, :, lanes]
            for moment in range(STEPS):
                value = value + tables[moment] * drawn[moment][:, 128 * t : 128 * (t + 1)]
            spec[s, :, lanes] = value
            feats[core, pl.ds(s * 32, 32), lanes] = value.astype(BF16)
        return carry

    lax.fori_loop(0, SHOTS, transform, 0)
    spectra_store = pltpu.make_async_copy(spec, spectra_out, out_sem.at[2])
    spectra_store.start()

    mate = {"shot": 2 * chip + 1 - core}
    feat_copy = pltpu.make_async_remote_copy(
        src_ref=feats.at[core],
        dst_ref=feats.at[core],
        send_sem=feat_send,
        recv_sem=feat_recv,
        device_id=mate,
        device_id_type=MESH,
    )
    feat_copy.start()
    feat_copy.wait_recv()

    blocks = [
        feats[:, :, pl.ds(pl.multiple_of(lax.rem(core + k, 4) * 128, 128), 128)].reshape(512, 128)
        for k in range(4)
    ]
    products = []
    for left, right in (((0), (0, 1, 2)), ((2), (2, 3))):
        product = lax.dot_general(
            blocks[left],
            jnp.concatenate([blocks[k] for k in right], axis=1),
            (((0,), (0,)), ((), ())),
            preferred_element_type=F32,
        )
        products += [product[:, 128 * k : 128 * (k + 1)] for k in range(len(right))]

    for k in range(5):
        half[pl.ds(128 * k, 128)] = products[k]

    def rows_of(place):
        return pl.ds(pl.multiple_of(place * CHUNK, 8), CHUNK)

    def part_copy(place):
        return pltpu.make_async_remote_copy(
            src_ref=half.at[rows_of(place)],
            dst_ref=part_in.at[chip],
            send_sem=part_send.at[place],
            recv_sem=part_recv.at[chip],
            device_id={"shot": 2 * place + core},
            device_id_type=MESH,
        )

    def part_arrival(place):
        return pltpu.make_async_remote_copy(
            src_ref=half.at[rows_of(place)],
            dst_ref=part_in.at[place],
            send_sem=part_send.at[place],
            recv_sem=part_recv.at[place],
            device_id={"shot": 2 * place + core},
            device_id_type=MESH,
        )

    for hop in FAR_FIRST:
        part_copy(lax.rem(chip + hop, CHIPS)).start()
    total = half[rows_of(chip)]
    for hop in NEAR_FIRST:
        place = lax.rem(chip + hop, CHIPS)
        part_arrival(place).wait_recv()
        total = total + part_in[place]
    gathered[core, rows_of(chip)] = total

    def ring_copy(owner, place):
        return pltpu.make_async_remote_copy(
            src_ref=gathered.at[core, rows_of(owner)],
            dst_ref=gathered.at[core, rows_of(owner)],
            send_sem=ring_send.at[place],
            recv_sem=ring_recv.at[owner],
            device_id={"shot": 2 * place + core},
            device_id_type=MESH,
        )

    def pass_copy(owner, which):
        return pltpu.make_async_remote_copy(
            src_ref=gathered.at[which, rows_of(owner)],
            dst_ref=gathered.at[which, rows_of(owner)],
            send_sem=pass_send.at[owner],
            recv_sem=pass_recv.at[owner],
            device_id=mate,
            device_id_type=MESH,
        )

    for hop in FAR_FIRST:
        ring_copy(chip, lax.rem(chip + hop, CHIPS)).start()
    pass_copy(chip, core).start()

    own_lists = lists_ref[shot]
    chosen = jnp.concatenate(
        [
            (lax.broadcasted_iota(jnp.int32, (512, PATCH), 0) == own_lists[p : p + 1])
            .astype(F32)
            .astype(BF16)
            for p in range(P_MAX)
        ],
        axis=1,
    )

    for hop in NEAR_FIRST:
        place = lax.rem(chip + hop, CHIPS)
        ring_copy(place, place).wait_recv()
        pass_copy(place, core).start()
    for hop in (0,) + NEAR_FIRST:
        pass_copy(lax.rem(chip + hop, CHIPS), 1 - core).wait_recv()

    strips = [None] * 4
    for which in range(2):
        grid = [gathered[which, pl.ds(128 * k, 128)] for k in range(5)]
        rows = [chosen[128 * (k % 4) : 128 * (k % 4 + 1)] for k in range(which, which + 4)]
        for row, left, right in (
            (which, [0.5 * grid[0], grid[1], grid[2]], rows[0:3]),
            (which + 2, [0.5 * grid[3], grid[4]], rows[2:4]),
        ):
            high, low = split(jnp.concatenate(left, axis=1))
            right = jnp.concatenate(right, axis=0)
            strips[row] = jnp.dot(high, right, preferred_element_type=F32) + jnp.dot(
                low, right, preferred_element_type=F32
            )
    strip_high, strip_low = split(jnp.concatenate(strips, axis=0))
    for p in range(P_MAX):
        lanes = slice(PATCH * p, PATCH * (p + 1))
        dims = (((0,), (0,)), ((), ()))
        tile = lax.dot_general(
            chosen[:, lanes], strip_high[:, lanes], dims, preferred_element_type=F32
        ) + lax.dot_general(
            chosen[:, lanes], strip_low[:, lanes], dims, preferred_element_type=F32
        )
        live = (counts_ref[0, 0] > p).astype(F32) * (1.0 / (2 * CHIPS * SHOTS * 32))
        gram_ref[p] = (tile + tile.T) * live

    for side, there in ((0, has_left), (1, has_right)):

        @pl.when(there)
        def _():
            for copy in halo_copies(side):
                copy.wait_send()

    feat_copy.wait_send()
    for hop in FAR_FIRST:
        place = lax.rem(chip + hop, CHIPS)
        part_copy(place).wait_send()
        ring_copy(chip, place).wait_send()
    for hop in (0,) + NEAR_FIRST:
        pass_copy(lax.rem(chip + hop, CHIPS), core).wait_send()
    for store in stores:
        store.wait()
    spectra_store.wait()


def shards(
    bricks,
    pressure,
    auxiliary,
    pressure_prior,
    auxiliary_prior,
    courant_sq,
    thomsen_epsilon,
    thomsen_delta,
    tilt_angle,
    frequencies,
    spectra,
    target_cells,
    patch_lists,
    patch_counts,
):
    vmem = pl.BlockSpec(memory_space=pltpu.VMEM)
    smem = pl.BlockSpec(memory_space=pltpu.SMEM)
    whole = pl.BlockSpec(memory_space=pl.ANY)
    field = jax.ShapeDtypeStruct((SHOTS, ROWS, DEPTH), F32)
    dma = pltpu.SemaphoreType.DMA
    p_out, q_out, spectra_out, gram = pl.pallas_call(
        functools.partial(kernel, bricks),
        out_shape=(field, field, field, jax.ShapeDtypeStruct((P_MAX, PATCH, PATCH), F32)),
        in_specs=[smem, smem] + [vmem] * 6 + [whole] * 5,
        out_specs=(whole, whole, whole, vmem),
        scratch_shapes=[
            pltpu.VMEM((STEPS + 2, ROWS + 2 * HALO, SHOTS, DEPTH), F32),
            pltpu.VMEM((STEPS + 2, ROWS + 2 * HALO, SHOTS, DEPTH), F32),
            pltpu.VMEM((5, ROWS + 16, DEPTH), F32),
            pltpu.VMEM((2, 7, 16, DEPTH), BF16),
            pltpu.VMEM((2, 7, 16, DEPTH), BF16),
            pltpu.VMEM((2, 16, DEPTH), F32),
            pltpu.VMEM((2, 16, DEPTH), F32),
            pltpu.VMEM((SHOTS, 32, DEPTH), F32),
            pltpu.VMEM((DEPTH, DEPTH), BF16),
            pltpu.VMEM((STEPS, SHOTS, DEPTH), F32),
            pltpu.VMEM((2, SHOTS * 32, DEPTH), BF16),
            pltpu.VMEM((CHIPS * CHUNK, 128), F32),
            pltpu.VMEM((CHIPS, CHUNK, 128), F32),
            pltpu.VMEM((2, CHIPS * CHUNK, 128), F32),
            dma((5,)),
            dma((3,)),
            dma((2, 2)),
            dma((2, 2)),
            dma,
            dma,
            dma((CHIPS,)),
            dma((CHIPS,)),
            dma((CHIPS,)),
            dma((CHIPS,)),
            dma((CHIPS,)),
            dma((CHIPS,)),
        ],
        compiler_params=pltpu.CompilerParams(collective_id=0, has_side_effects=True),
    )(
        frequencies,
        patch_counts,
        courant_sq,
        thomsen_epsilon,
        thomsen_delta,
        tilt_angle,
        target_cells.reshape(1, -1),
        patch_lists[0],
        pressure,
        auxiliary,
        pressure_prior,
        auxiliary_prior,
        spectra,
    )
    return p_out, q_out, spectra_out, gram.reshape(1, 1, P_MAX, PATCH, PATCH)


def solution(mesh):
    return jax.shard_map(
        functools.partial(shards, mesh.shape["brick"]),
        mesh=mesh,
        in_specs=(
            P("shot", "brick", None),
            P("shot", "brick", None),
            P("shot", "brick", None),
            P("shot", "brick", None),
            P("brick", None),
            P("brick", None),
            P("brick", None),
            P("brick", None),
            P(),
            P("shot", None, "brick"),
            P("brick"),
            P("brick", None, None, None),
            P("brick", "shot"),
        ),
        out_specs=(
            P("shot", "brick", None),
            P("shot", "brick", None),
            P("shot", None, "brick"),
            P("brick", "shot", None, None, None),
        ),
        check_vma=False,
    )
```

time: 158 us -> 59.1 us (0.37); the launches traced: 155 us -> 58.7 us
  waiting for transfers between devices: 56.8 us -> 0 us
  Pallas kernels: 0 us -> 51.1 us
  local copies, waits for them, and re-layouts: 50 us -> 6.32 us
  other arithmetic: 16 us -> 0 us
  between operations: 15.1 us -> 1.3 us
  starting transfers between devices: 12.9 us -> 0 us
  matrix products: 4.63 us -> 0 us
    all_gather x1 -> x0, waiting for transfers between devices: 51.4 us -> none  [shards(): portion = lax.all_gather(features, 'shot', axis=0, tiled=True)]
    pallas_call x0 -> x1, Pallas kernels: none -> 51.1 us  [shards(): pl.pallas_call(functools.partial(kernel, bricks), out_shape=(field, field...]
    gather x5 -> x0, local copies, waits for them, and re-layouts: 28.6 us -> none  [the longest x4 17.7 us: shards(): jnp.take(interior.reshape(shots_here, width_x * depth), target_cells, axi...]
    slice x9 -> x0, local copies, waits for them, and re-layouts: 14.6 us -> none  [the longest x4 9.44 us: shards(): interior = current[0][:, margin:margin + width_x]]
    ppermute x2 -> x0, starting transfers between devices: 12.9 us -> none  [the longest x1 8.85 us: with_halo(): lax.ppermute(head, axis, [((i + 1) % count, i) for i in range(ends)])]
    add x9 -> x0, other arithmetic: 10.4 us -> none  [the longest x4 5.53 us: leapfrog(): 2.0 * auxiliary - former[1]]
    unnamed x20 -> x11, local copies, waits for them, and re-layouts: 0.9 us -> 6.32 us
    ppermute x2 -> x0, waiting for transfers between devices: 5.34 us -> none  [the longest x1 4.44 us: with_halo(): lax.ppermute(tail, axis, [(i, (i + 1) % count) for i in range(ends)])]
  transfers between devices with their start and end apart: 3 -> 0, of which waited for: 3 -> 0; matrix products, arithmetic and copies ran while one was open for 1% -> 0% of each run, Pallas kernels for 0% -> 0%
where the time goes in v1:
time: 59.1 us; the launch traced here: 58.7 us
  Pallas kernels  51.1 us (86%)
  local copies, waits for them, and re-layouts  6.32 us (11%)
  between operations  1.3 us (2%)
    pallas_call x1, Pallas kernels, shards(): pl.pallas_call(functools.partial(kernel, bricks), out_shape=(field, field...  51.1 us
    unnamed x11, local copies, waits for them, and re-layouts  6.32 us

profile of v1, /device:TPU:7, one launch (start us, length us, event | category | flops | bytes accessed | tf_op | source)
XLA Modules:
  0.0 58.7 jit_solution(6325183519376439308)
XLA Ops:
  1.3 1.4 %copy.19 = s32[1,16,3,128]{3,2,1,0:T(4,128)} copy(s32[1,16,3,128]{3,1,2,0:T(8,128)} %param.24) | data formatting | bytes 49152 | tf_op args[11]
  2.6 51.1 %shard_map.156 = (f32[8,32,512]{2,1,0:T(8,128)}, f32[8,32,512]{2,1,0:T(8,128)}, f32[8,32,512]{2,1,0:T(8,128)}, f32[3,128,128]{2,1,0:T(8,128)}) custom-call(f32[16]{0:T(128)} %freq_ref.1, s32[1,1]{1,0:T(1,128)S(6)} %copy.24.counts_ref, f32[32,512]{1,0:T(8,128)} %courant_ref.1, f32[32,512]{1,0:T(8,128)} %epsilon_ref.1, f32[32,512]{1,0:T(8,128)} %delta_ref.1, ...), custom_call_target="tpu_custom_call" | custom-call | tf_op jit(solution)/shard_map/pallas_call | solution.py:516
  53.7 0.0 copy-start.1
  53.7 1.9 %copy.25 = f32[8,32,512]{2,1,0:T(8,128)} copy(f32[8,32,512]{2,1,0:T(8,128)} %get-tuple-element.16) | data formatting | bytes 1048576
  55.7 0.0 copy-done.1
  55.7 0.0 copy-start
  55.7 0.8 %copy.26 = f32[8,32,512]{2,1,0:T(8,128)} copy(f32[8,32,512]{2,1,0:T(8,128)S(1)} %copy-done.1) | data formatting | bytes 1048576
  56.5 0.4 copy-done
  56.9 0.0 copy-start.2
  56.9 0.8 %copy.27 = f32[8,32,512]{2,1,0:T(8,128)} copy(f32[8,32,512]{2,1,0:T(8,128)S(1)} %copy-done) | data formatting | bytes 1048576
  57.7 0.3 copy-done.2
  58.0 0.7 %copy.28 = f32[1,1,3,128,128]{4,3,2,1,0:T(8,128)} copy(f32[1,1,3,128,128]{4,3,2,1,0:T(8,128)S(1)} %bitcast.5) | data formatting | bytes 393216
Async XLA Ops:
  53.7 1.9 %copy-start.1 = (f32[8,32,512]{2,1,0:T(8,128)S(1)}, f32[8,32,512]{2,1,0:T(8,128)}, u32[]{:S(2)}) copy-start(f32[8,32,512]{2,1,0:T(8,128)} %get-tuple-element.17) | copy-start | bytes 1572868
  55.7 1.2 %copy-start = (f32[8,32,512]{2,1,0:T(8,128)S(1)}, f32[8,32,512]{2,1,0:T(8,128)}, u32[]{:S(2)}) copy-start(f32[8,32,512]{2,1,0:T(8,128)} %get-tuple-element.18) | copy-start | bytes 1572868
  56.9 1.1 %copy-start.2 = (f32[3,128,128]{2,1,0:T(8,128)S(1)}, f32[3,128,128]{2,1,0:T(8,128)}, u32[]{:S(2)}) copy-start(f32[3,128,128]{2,1,0:T(8,128)} %get-tuple-element.11) | copy-start | bytes 589828

commit v2 on v1

--- a/solution.py
+++ b/solution.py
@@ -16,7 +16,8 @@
 DEPTH = 512
 TILES = DEPTH // 128
 CHIPS = 8
-CHUNK = 80
+CHUNK = 128 // CHIPS
+FULL = 178.0
 MESH = pl.DeviceIdType.MESH
 F32 = jnp.float32
 BF16 = jnp.bfloat16
@@ -45,30 +46,30 @@
     pp_in,
     qq_in,
     spectra_in,
-    p_out,
-    q_out,
-    spectra_out,
-    gram_ref,
     pbuf,
     qbuf,
+    spec,
+    gram_ref,
     coef,
     slab_out,
     slab_in,
     rim_out,
     rim_in,
-    spec,
     onehot,
     samples,
     feats,
+    energy,
     half,
+    part_out,
     part_in,
     gathered,
     in_sem,
-    out_sem,
     halo_send,
     halo_recv,
     feat_send,
     feat_recv,
+    energy_send,
+    energy_recv,
     part_send,
     part_recv,
     ring_send,
@@ -122,15 +123,15 @@
     courant = courant_ref[...]
     own = pl.ds(8, ROWS)
     coef[0, own] = cosine * cosine
-    coef[1, own] = 0.5 * sine * cosine
-    coef[2, own] = courant
-    coef[3, own] = courant * (1.0 + 2.0 * epsilon_ref[...])
-    coef[4, own] = courant * (1.0 + 2.0 * delta_ref[...])
-    for number in range(5):
-        rim_out[0, pl.ds(3 * number, 3)] = coef[number, pl.ds(8, 3)]
-        rim_out[1, pl.ds(3 * number, 3)] = coef[number, pl.ds(8 + ROWS - 3, 3)]
-    rim_out[0, pl.ds(15, 1)] = jnp.zeros((1, DEPTH), F32)
-    rim_out[1, pl.ds(15, 1)] = jnp.zeros((1, DEPTH), F32)
+    coef[1, own] = sine * sine
+    coef[2, own] = 0.5 * sine * cosine
+    coef[3, own] = courant
+    coef[4, own] = courant * (1.0 + 2.0 * epsilon_ref[...])
+    coef[5, own] = courant * (1.0 + 2.0 * delta_ref[...])
+    for number in range(6):
+        rim_out[0, pl.ds(4 * number, 3)] = coef[number, pl.ds(8, 3)]
+        rim_out[1, pl.ds(4 * number, 3)] = coef[number, pl.ds(8 + ROWS - 3, 3)]
+        rim_out[:, pl.ds(4 * number + 3, 1)] = jnp.zeros((2, 1, DEPTH), F32)
 
     for load in loads:
         load.wait()
@@ -201,14 +202,14 @@
         cross = [a - b for a, b in zip(deeper(slope), shallower(slope))]
         return steep, deep, cross
 
-    def two_rows(moment, row):
-        p_rows = [tiles(pbuf[moment, row + k]) for k in range(-1, 3)]
-        q_rows = [tiles(qbuf[moment, row + k]) for k in range(-1, 3)]
-        for k in range(2):
+    def some_rows(moment, row, count):
+        p_rows = [tiles(pbuf[moment, row + k]) for k in range(-1, count + 1)]
+        q_rows = [tiles(qbuf[moment, row + k]) for k in range(-1, count + 1)]
+        for k in range(count):
             at = row + k
-            cos_sq, twist, speed, speed_e, speed_d = (
+            cos_sq, sin_sq, twist, speed, speed_e, speed_d = (
                 tiles(jnp.broadcast_to(coef[number, pl.ds(at + 4, 1)], (SHOTS, DEPTH)))
-                for number in range(5)
+                for number in range(6)
             )
             p_steep, p_deep, p_cross = stencil(p_rows[k], p_rows[k + 1], p_rows[k + 2])
             q_steep, q_deep, q_cross = stencil(q_rows[k], q_rows[k + 1], q_rows[k + 2])
@@ -217,20 +218,23 @@
             for t in range(TILES):
                 p_two = p_rows[k + 1][t] + p_rows[k + 1][t]
                 q_two = q_rows[k + 1][t] + q_rows[k + 1][t]
-                sin_sq = 1.0 - cos_sq[t]
-                across = cos_sq[t] * p_steep[t] + sin_sq * p_deep[t] - twist[t] * p_cross[t] - p_two
-                along = sin_sq * q_steep[t] + cos_sq[t] * q_deep[t] + twist[t] * q_cross[t] - q_two
+                across = (
+                    cos_sq[t] * p_steep[t] + sin_sq[t] * p_deep[t] - twist[t] * p_cross[t] - p_two
+                )
+                along = (
+                    sin_sq[t] * q_steep[t] + cos_sq[t] * q_deep[t] + twist[t] * q_cross[t] - q_two
+                )
                 push = speed[t] * along
                 lanes = pl.ds(128 * t, 128)
                 pbuf[moment + 1, at, :, lanes] = (p_two - p_old[t]) + (speed_e[t] * across + push)
                 qbuf[moment + 1, at, :, lanes] = (q_two - q_old[t]) + (speed_d[t] * across + push)
 
     def inner_step(moment, carry):
-        def pair(number, carry):
-            two_rows(moment, moment + HALO + 2 * number)
+        def group(number, carry):
+            some_rows(moment, moment + HALO + 4 * number, 4)
             return carry
 
-        return lax.fori_loop(0, ROWS // 2 - moment, pair, carry)
+        return lax.fori_loop(0, (ROWS - 2 * moment + 3) // 4, group, carry)
 
     lax.fori_loop(1, STEPS + 1, inner_step, 0)
 
@@ -279,7 +283,7 @@
         @pl.when(jnp.logical_not(there))
         def _():
             slab_in[side] = jnp.zeros((7, 16, DEPTH), BF16)
-            rim_in[side] = jnp.zeros((16, DEPTH), F32)
+            rim_in[side] = jnp.zeros((24, DEPTH), F32)
 
     for side in range(2):
         first = 0 if side == 0 else HALO + ROWS
@@ -292,41 +296,37 @@
             both = slab_in[side, 4 + row].astype(F32)
             pbuf[0, first + row] = both[:SHOTS]
             qbuf[0, first + row] = both[SHOTS:]
-        for k in range(5):
-            coef[k, pl.ds(first + 4, 3)] = rim_in[side, pl.ds(3 * k, 3)]
+        for k in range(6):
+            coef[k, pl.ds(first + 4, 3)] = rim_in[side, pl.ds(4 * k, 3)]
 
     def outer_step(moment, carry):
-        def pair(number, carry):
-            two_rows(
-                moment,
-                jnp.where(number < 2, moment + 2 * number, ROWS - moment + 2 * number),
-            )
+        def group(side, carry):
+            some_rows(moment, jnp.where(side == 0, moment, HALO + ROWS - moment), 4)
             return carry
 
-        return lax.fori_loop(0, 4, pair, carry)
+        return lax.fori_loop(0, 2, group, carry)
 
     lax.fori_loop(1, STEPS + 1, outer_step, 0)
 
-    stores = []
-    for number, (source, target) in enumerate(((pbuf, p_out), (qbuf, q_out))):
-        for s in range(SHOTS):
-            stores.append(
-                pltpu.make_async_copy(
-                    source.at[STEPS + 1, pl.ds(HALO, ROWS), s],
-                    target.at[s],
-                    out_sem.at[number],
-                )
-            )
-    for store in stores:
-        store.start()
-
-    def outer_samples(moment, carry):
-        samples[moment - 1] = (
-            samples[moment - 1] + picked(moment, 0, HALO) + picked(moment, ROWS - HALO, HALO)
-        )
-        return carry
-
-    lax.fori_loop(1, STEPS + 1, outer_samples, 0)
+    edges = jnp.concatenate(
+        [
+            pbuf[moment + 1, pl.ds(first + HALO, HALO)].reshape(HALO * SHOTS, DEPTH)
+            for moment in range(1, STEPS + 1)
+            for first in (0, ROWS - HALO)
+        ],
+        axis=0,
+    )
+    high, low = split(edges)
+    values = jnp.dot(high, onehot[...], preferred_element_type=F32) + jnp.dot(
+        low, onehot[...], preferred_element_type=F32
+    )
+    for moment in range(STEPS):
+        total = samples[moment]
+        for k in range(2 * HALO):
+            x = k if k < HALO else ROWS - 2 * HALO + k
+            start = (moment * 2 * HALO + k) * SHOTS
+            total = total + jnp.where(target_x == x, values[start : start + SHOTS], 0.0)
+        samples[moment] = total
 
     spectra_load.wait()
 
@@ -342,8 +342,6 @@
         return carry
 
     lax.fori_loop(0, SHOTS, transform, 0)
-    spectra_store = pltpu.make_async_copy(spec, spectra_out, out_sem.at[2])
-    spectra_store.start()
 
     mate = {"shot": 2 * chip + 1 - core}
     feat_copy = pltpu.make_async_remote_copy(
@@ -357,59 +355,104 @@
     feat_copy.start()
     feat_copy.wait_recv()
 
+    both = feats[...].reshape(2 * SHOTS * 32, DEPTH)
+    energy[chip] = jnp.dot(
+        jnp.ones((8, 2 * SHOTS * 32), BF16), both * both, preferred_element_type=F32
+    )
+
+    def energy_copy(place, owner):
+        return pltpu.make_async_remote_copy(
+            src_ref=energy.at[owner, pl.ds(0, 1)],
+            dst_ref=energy.at[owner, pl.ds(0, 1)],
+            send_sem=energy_send.at[place],
+            recv_sem=energy_recv.at[owner],
+            device_id={"shot": 2 * place + core},
+            device_id_type=MESH,
+        )
+
+    for hop in FAR_FIRST:
+        energy_copy(lax.rem(chip + hop, CHIPS), chip).start()
+
+    def units(place):
+        level = energy[place, pl.ds(0, 1)]
+        inverse = jnp.where(level > 0.0, lax.rsqrt(level), 0.0)
+        return level * inverse, inverse
+
+    def in_order(row):
+        straight = [row[:, 128 * k : 128 * (k + 1)] for k in range(4)]
+        return [jnp.where(core == 0, straight[k], straight[(k + 1) % 4]) for k in range(4)]
+
+    pairs = ((0, 0), (0, 1), (0, 2), (2, 2), (2, 3))
     blocks = [
         feats[:, :, pl.ds(pl.multiple_of(lax.rem(core + k, 4) * 128, 128), 128)].reshape(512, 128)
         for k in range(4)
     ]
-    products = []
-    for left, right in (((0), (0, 1, 2)), ((2), (2, 3))):
+    row_number = lax.broadcasted_iota(jnp.int32, (128, 128), 0)
+    lane_number = lax.broadcasted_iota(jnp.int32, (128, 128), 1)
+
+    def upright(row, first, count):
+        here = lane_number[:count] == row_number[:count] + first
+        return jnp.sum(jnp.where(here, row, 0.0), axis=1, keepdims=True)
+
+    inverses = in_order(units(chip)[1])
+    columns = {k: upright(inverses[k] * FULL, 0, 128) for k in (0, 2)}
+    number = 0
+    for left, right in ((0, (0, 1, 2)), (2, (2, 3))):
         product = lax.dot_general(
             blocks[left],
             jnp.concatenate([blocks[k] for k in right], axis=1),
             (((0,), (0,)), ((), ())),
             preferred_element_type=F32,
         )
-        products += [product[:, 128 * k : 128 * (k + 1)] for k in range(len(right))]
-
-    for k in range(5):
-        half[pl.ds(128 * k, 128)] = products[k]
+        for k, block in enumerate(right):
+            value = product[:, 128 * k : 128 * (k + 1)]
+            half[number] = value
+            part_out[number] = jnp.round(value * columns[left] * (inverses[block] * FULL)).astype(jnp.int16)
+            number += 1
 
     def rows_of(place):
-        return pl.ds(pl.multiple_of(place * CHUNK, 8), CHUNK)
-
-    def part_copy(place):
+        return pl.ds(pl.multiple_of(place * CHUNK, CHUNK), CHUNK)
+
+    def part_copy(place, owner):
         return pltpu.make_async_remote_copy(
-            src_ref=half.at[rows_of(place)],
-            dst_ref=part_in.at[chip],
+            src_ref=part_out.at[:, rows_of(place)],
+            dst_ref=part_in.at[owner],
             send_sem=part_send.at[place],
-            recv_sem=part_recv.at[chip],
+            recv_sem=part_recv.at[owner],
             device_id={"shot": 2 * place + core},
             device_id_type=MESH,
         )
 
-    def part_arrival(place):
-        return pltpu.make_async_remote_copy(
-            src_ref=half.at[rows_of(place)],
-            dst_ref=part_in.at[place],
-            send_sem=part_send.at[place],
-            recv_sem=part_recv.at[place],
-            device_id={"shot": 2 * place + core},
-            device_id_type=MESH,
-        )
-
     for hop in FAR_FIRST:
-        part_copy(lax.rem(chip + hop, CHIPS)).start()
-    total = half[rows_of(chip)]
+        part_copy(lax.rem(chip + hop, CHIPS), chip).start()
+
+    start = chip * CHUNK
+    total = [half[k, rows_of(chip)] for k in range(5)]
     for hop in NEAR_FIRST:
         place = lax.rem(chip + hop, CHIPS)
-        part_arrival(place).wait_recv()
-        total = total + part_in[place]
-    gathered[core, rows_of(chip)] = total
+        energy_copy(place, place).wait_recv()
+        roots = in_order(units(place)[0])
+        columns = {k: upright(roots[k] * (1.0 / FULL), start, CHUNK) for k in (0, 2)}
+        part_copy(place, place).wait_recv()
+        for k, (left, right) in enumerate(pairs):
+            total[k] = total[k] + part_in[place, k].astype(F32) * columns[left] * (roots[right] * (1.0 / FULL))
+
+    level = energy[0, pl.ds(0, 1)]
+    for k in range(1, CHIPS):
+        level = level + energy[k, pl.ds(0, 1)]
+    inverse = jnp.where(level > 0.0, lax.rsqrt(level), 0.0)
+    root = level * inverse
+    inverses = in_order(inverse)
+    columns = {k: upright(inverses[k] * FULL, start, CHUNK) for k in (0, 2)}
+    for k, (left, right) in enumerate(pairs):
+        gathered[core, k, rows_of(chip)] = jnp.round(
+            total[k] * columns[left] * (inverses[right] * FULL)
+        ).astype(jnp.int16)
 
     def ring_copy(owner, place):
         return pltpu.make_async_remote_copy(
-            src_ref=gathered.at[core, rows_of(owner)],
-            dst_ref=gathered.at[core, rows_of(owner)],
+            src_ref=gathered.at[core, :, rows_of(owner)],
+            dst_ref=gathered.at[core, :, rows_of(owner)],
             send_sem=ring_send.at[place],
             recv_sem=ring_recv.at[owner],
             device_id={"shot": 2 * place + core},
@@ -418,8 +461,8 @@
 
     def pass_copy(owner, which):
         return pltpu.make_async_remote_copy(
-            src_ref=gathered.at[which, rows_of(owner)],
-            dst_ref=gathered.at[which, rows_of(owner)],
+            src_ref=gathered.at[which, :, rows_of(owner)],
+            dst_ref=gathered.at[which, :, rows_of(owner)],
             send_sem=pass_send.at[owner],
             recv_sem=pass_recv.at[owner],
             device_id=mate,
@@ -430,10 +473,9 @@
         ring_copy(chip, lax.rem(chip + hop, CHIPS)).start()
     pass_copy(chip, core).start()
 
-    own_lists = lists_ref[shot]
     chosen = jnp.concatenate(
         [
-            (lax.broadcasted_iota(jnp.int32, (512, PATCH), 0) == own_lists[p : p + 1])
+            (lax.broadcasted_iota(jnp.int32, (512, PATCH), 0) == lists_ref[p, pl.ds(shot, 1)])
             .astype(F32)
             .astype(BF16)
             for p in range(P_MAX)
@@ -450,7 +492,7 @@
 
     strips = [None] * 4
     for which in range(2):
-        grid = [gathered[which, pl.ds(128 * k, 128)] for k in range(5)]
+        grid = [gathered[which, k].astype(F32) for k in range(5)]
         rows = [chosen[128 * (k % 4) : 128 * (k % 4 + 1)] for k in range(which, which + 4)]
         for row, left, right in (
             (which, [0.5 * grid[0], grid[1], grid[2]], rows[0:3]),
@@ -462,6 +504,10 @@
                 low, right, preferred_element_type=F32
             )
     strip_high, strip_low = split(jnp.concatenate(strips, axis=0))
+    root_high, root_low = split(jnp.broadcast_to(root * (1.0 / FULL), (8, DEPTH)))
+    chosen_root = jnp.dot(root_high, chosen, preferred_element_type=F32) + jnp.dot(
+        root_low, chosen, preferred_element_type=F32
+    )
     for p in range(P_MAX):
         lanes = slice(PATCH * p, PATCH * (p + 1))
         dims = (((0,), (0,)), ((), ()))
@@ -471,7 +517,8 @@
             chosen[:, lanes], strip_low[:, lanes], dims, preferred_element_type=F32
         )
         live = (counts_ref[0, 0] > p).astype(F32) * (1.0 / (2 * CHIPS * SHOTS * 32))
-        gram_ref[p] = (tile + tile.T) * live
+        scale = chosen_root[0:1, lanes]
+        gram_ref[p] = ((tile + tile.T) * scale).T * (scale * live)
 
     for side, there in ((0, has_left), (1, has_right)):
 
@@ -483,13 +530,29 @@
     feat_copy.wait_send()
     for hop in FAR_FIRST:
         place = lax.rem(chip + hop, CHIPS)
-        part_copy(place).wait_send()
+        energy_copy(place, chip).wait_send()
+        part_copy(place, chip).wait_send()
         ring_copy(chip, place).wait_send()
     for hop in (0,) + NEAR_FIRST:
         pass_copy(lax.rem(chip + hop, CHIPS), core).wait_send()
-    for store in stores:
-        store.wait()
-    spectra_store.wait()
+
+
+def deliver(pbuf, qbuf, spec, gram, p_out, q_out, spectra_out, gram_out, sem):
+    copies = [
+        pltpu.make_async_copy(spec, spectra_out, sem.at[2]),
+        pltpu.make_async_copy(gram, gram_out, sem.at[3]),
+    ]
+    for number, (source, target) in enumerate(((pbuf, p_out), (qbuf, q_out))):
+        for s in range(SHOTS):
+            copies.append(
+                pltpu.make_async_copy(
+                    source.at[STEPS + 1, pl.ds(HALO, ROWS), s], target.at[s], sem.at[number]
+                )
+            )
+    for copy in copies:
+        copy.start()
+    for copy in copies:
+        copy.wait()
 
 
 def shards(
@@ -510,31 +573,34 @@
 ):
     vmem = pl.BlockSpec(memory_space=pltpu.VMEM)
     smem = pl.BlockSpec(memory_space=pltpu.SMEM)
-    whole = pl.BlockSpec(memory_space=pl.ANY)
-    field = jax.ShapeDtypeStruct((SHOTS, ROWS, DEPTH), F32)
+    whole = pl.BlockSpec(memory_space=pltpu.HBM)
+    history = pltpu.VMEM((STEPS + 2, ROWS + 2 * HALO, SHOTS, DEPTH), F32)
     dma = pltpu.SemaphoreType.DMA
-    p_out, q_out, spectra_out, gram = pl.pallas_call(
+    made = pl.pallas_call(
         functools.partial(kernel, bricks),
-        out_shape=(field, field, field, jax.ShapeDtypeStruct((P_MAX, PATCH, PATCH), F32)),
+        out_shape=(
+            history,
+            history,
+            pltpu.VMEM((SHOTS, 32, DEPTH), F32),
+            pltpu.VMEM((P_MAX, PATCH, PATCH), F32),
+        ),
         in_specs=[smem, smem] + [vmem] * 6 + [whole] * 5,
-        out_specs=(whole, whole, whole, vmem),
+        out_specs=(vmem,) * 4,
         scratch_shapes=[
-            pltpu.VMEM((STEPS + 2, ROWS + 2 * HALO, SHOTS, DEPTH), F32),
-            pltpu.VMEM((STEPS + 2, ROWS + 2 * HALO, SHOTS, DEPTH), F32),
-            pltpu.VMEM((5, ROWS + 16, DEPTH), F32),
+            pltpu.VMEM((6, ROWS + 16, DEPTH), F32),
             pltpu.VMEM((2, 7, 16, DEPTH), BF16),
             pltpu.VMEM((2, 7, 16, DEPTH), BF16),
-            pltpu.VMEM((2, 16, DEPTH), F32),
-            pltpu.VMEM((2, 16, DEPTH), F32),
-            pltpu.VMEM((SHOTS, 32, DEPTH), F32),
+            pltpu.VMEM((2, 24, DEPTH), F32),
+            pltpu.VMEM((2, 24, DEPTH), F32),
             pltpu.VMEM((DEPTH, DEPTH), BF16),
             pltpu.VMEM((STEPS, SHOTS, DEPTH), F32),
             pltpu.VMEM((2, SHOTS * 32, DEPTH), BF16),
-            pltpu.VMEM((CHIPS * CHUNK, 128), F32),
-            pltpu.VMEM((CHIPS, CHUNK, 128), F32),
-            pltpu.VMEM((2, CHIPS * CHUNK, 128), F32),
+            pltpu.VMEM((CHIPS, 8, DEPTH), F32),
+            pltpu.VMEM((5, 128, 128), F32),
+            pltpu.VMEM((5, 128, 128), jnp.int16),
+            pltpu.VMEM((CHIPS, 5, CHUNK, 128), jnp.int16),
+            pltpu.VMEM((2, 5, 128, 128), jnp.int16),
             dma((5,)),
-            dma((3,)),
             dma((2, 2)),
             dma((2, 2)),
             dma,
@@ -545,8 +611,12 @@
             dma((CHIPS,)),
             dma((CHIPS,)),
             dma((CHIPS,)),
+            dma((CHIPS,)),
+            dma((CHIPS,)),
         ],
-        compiler_params=pltpu.CompilerParams(collective_id=0, has_side_effects=True),
+        compiler_params=pltpu.CompilerParams(
+            collective_id=0, has_side_effects=True, vmem_limit_bytes=50 << 20
+        ),
     )(
         frequencies,
         patch_counts,
@@ -555,13 +625,22 @@
         thomsen_delta,
         tilt_angle,
         target_cells.reshape(1, -1),
-        patch_lists[0],
+        jnp.transpose(patch_lists[0], (1, 0, 2)),
         pressure,
         auxiliary,
         pressure_prior,
         auxiliary_prior,
         spectra,
     )
+    field = jax.ShapeDtypeStruct((SHOTS, ROWS, DEPTH), F32)
+    p_out, q_out, spectra_out, gram = pl.pallas_call(
+        deliver,
+        out_shape=(field, field, field, jax.ShapeDtypeStruct((P_MAX, PATCH, PATCH), F32)),
+        in_specs=[vmem] * 4,
+        out_specs=(whole,) * 4,
+        scratch_shapes=[dma((4,))],
+        compiler_params=pltpu.CompilerParams(vmem_limit_bytes=8 << 20),
+    )(*(pltpu.with_memory_space_constraint(array, pltpu.VMEM) for array in made))
     return p_out, q_out, spectra_out, gram.reshape(1, 1, P_MAX, PATCH, PATCH)
 
 

time: 59.1 us -> 44.4 us (0.75)
  Pallas kernels: 51.1 us -> 42.9 us
  local copies, waits for them, and re-layouts: 6.32 us -> 0 us
    pallas_call x1 -> x2, Pallas kernels: 51.1 us -> 42.9 us  [the longest x1 41.7 us: shards(): pl.pallas_call(functools.partial(kernel, bricks), out_shape=(history, his...]
    unnamed x11 -> x0, local copies, waits for them, and re-layouts: 6.32 us -> none
where the time goes in v2:
time: 44.4 us; the launch traced here: 44.2 us
  Pallas kernels  42.9 us (97%)
  between operations  1.29 us (3%)
    pallas_call x1, Pallas kernels, shards(): pl.pallas_call(functools.partial(kernel, bricks), out_shape=(history, his...  41.7 us
    pallas_call x1, Pallas kernels, shards(): pl.pallas_call(deliver, out_shape=(field, field, field, jax.ShapeDtypeStr...  1.22 us

profile of v2, /device:TPU:7, one launch (start us, length us, event | category | flops | bytes accessed | tf_op | source)
XLA Modules:
  0.0 44.2 jit_solution(12922553889004912783)
XLA Ops:
  1.3 41.7 %shard_map.156 = (f32[6,40,8,512]{3,2,1,0:T(8,128)S(1)}, f32[6,40,8,512]{3,2,1,0:T(8,128)S(1)}, f32[8,32,512]{2,1,0:T(8,128)S(1)}, f32[3,128,128]{2,1,0:T(8,128)S(1)}) custom-call(f32[16]{0:T(128)} %freq_ref.1, s32[1,1]{1,0:T(1,128)S(6)} %copy.17.counts_ref, f32[32,512]{1,0:T(8,128)} %courant_ref.1, f32[32,512]{1,0:T(8,128)} %epsilon_ref.1, ...), custom_call_target="tpu_custom_call" | custom-call | tf_op jit(solution)/shard_map/pallas_call | solution.py:579
  43.0 1.2 %shard_map.157 = (f32[8,32,512]{2,1,0:T(8,128)}, f32[8,32,512]{2,1,0:T(8,128)}, f32[8,32,512]{2,1,0:T(8,128)}, f32[3,128,128]{2,1,0:T(8,128)}) custom-call(f32[6,40,8,512]{3,2,1,0:T(8,128)S(1)} %get-tuple-element.12.pbuf, f32[6,40,8,512]{3,2,1,0:T(8,128)S(1)} %get-tuple-element.13.qbuf, f32[8,32,512]{2,1,0:T(8,128)S(1)} %get-tuple-element.14.spec, ...), custom_call_target="tpu_custom_call" | custom-call | tf_op jit(solution)/shard_map/pallas_call | solution.py:636

commit v3 on v2

--- a/solution.py
+++ b/solution.py
@@ -35,10 +35,10 @@
     bricks,
     freq_ref,
     counts_ref,
-    courant_ref,
-    epsilon_ref,
-    delta_ref,
-    tilt_ref,
+    courant_in,
+    epsilon_in,
+    delta_in,
+    tilt_in,
     cells_ref,
     lists_ref,
     p_in,
@@ -50,12 +50,15 @@
     qbuf,
     spec,
     gram_ref,
+    model,
     coef,
     slab_out,
     slab_in,
     rim_out,
     rim_in,
     onehot,
+    chosen,
+    table,
     samples,
     feats,
     energy,
@@ -101,6 +104,12 @@
     def _():
         pl.semaphore_signal(barrier, inc=1, device_id={"brick": brick + 1}, device_id_type=MESH)
 
+    model_loads = [
+        pltpu.make_async_copy(source, model.at[k], in_sem.at[5])
+        for k, source in enumerate((courant_in, epsilon_in, delta_in, tilt_in))
+    ]
+    for load in model_loads:
+        load.start()
     loads = []
     for number, (source, target, slot) in enumerate(
         ((p_in, pbuf, 1), (q_in, qbuf, 1), (pp_in, pbuf, 0), (qq_in, qbuf, 0))
@@ -118,16 +127,49 @@
     spectra_load = pltpu.make_async_copy(spectra_in, spec, in_sem.at[4])
     spectra_load.start()
 
-    sine = jnp.sin(tilt_ref[...])
-    cosine = jnp.cos(tilt_ref[...])
-    courant = courant_ref[...]
+    cells = cells_ref[...]
+    target_x = cells >> 9
+    target_z = cells & (DEPTH - 1)
+    onehot[...] = (
+        lax.broadcasted_iota(jnp.int32, (DEPTH, DEPTH), 0) == target_z
+    ).astype(F32).astype(BF16)
+
+    for p in range(P_MAX):
+        chosen[:, pl.ds(PATCH * p, PATCH)] = (
+            (lax.broadcasted_iota(jnp.int32, (512, PATCH), 0) == lists_ref[p, pl.ds(shot, 1)])
+            .astype(F32)
+            .astype(BF16)
+        )
+
+    number = lax.broadcasted_iota(jnp.int32, (16, 128), 0)
+    frequency = jnp.zeros((16, 128), F32)
+    for k in range(16):
+        frequency = jnp.where(number == k, freq_ref[k], frequency)
+    for moment in range(STEPS):
+        angle = frequency * (moment + 1.0)
+        table[moment, pl.ds(0, 16)] = jnp.cos(angle)
+        table[moment, pl.ds(16, 16)] = -jnp.sin(angle)
+
+    def shifted(value):
+        lane = lax.broadcasted_iota(jnp.int32, value.shape, 1)
+        return (
+            jnp.where(lane == 0, 0.0, pltpu.roll(value, 1, 1)),
+            jnp.where(lane == DEPTH - 1, 0.0, pltpu.roll(value, DEPTH - 1, 1)),
+        )
+
+    for load in model_loads:
+        load.wait()
+    sine = jnp.sin(model[3])
+    cosine = jnp.cos(model[3])
+    courant = model[0]
     own = pl.ds(8, ROWS)
-    coef[0, own] = cosine * cosine
-    coef[1, own] = sine * sine
-    coef[2, own] = 0.5 * sine * cosine
+    turns = (cosine * cosine, sine * sine, 0.5 * sine * cosine)
+    for k, value in enumerate(turns):
+        coef[k, own] = value
+        coef[6 + k, own], coef[9 + k, own] = shifted(value)
     coef[3, own] = courant
-    coef[4, own] = courant * (1.0 + 2.0 * epsilon_ref[...])
-    coef[5, own] = courant * (1.0 + 2.0 * delta_ref[...])
+    coef[4, own] = courant * (1.0 + 2.0 * model[1])
+    coef[5, own] = courant * (1.0 + 2.0 * model[2])
     for number in range(6):
         rim_out[0, pl.ds(4 * number, 3)] = coef[number, pl.ds(8, 3)]
         rim_out[1, pl.ds(4 * number, 3)] = coef[number, pl.ds(8 + ROWS - 3, 3)]
@@ -188,42 +230,53 @@
 
     def deeper(value):
         turned = [pltpu.roll(tile, 127, 1) for tile in value]
-        turned.append(jnp.zeros((SHOTS, 128), F32))
-        return [jnp.where(last_lane, turned[k + 1], turned[k]) for k in range(TILES)]
+        return [jnp.where(last_lane, turned[(k + 1) % TILES], turned[k]) for k in range(TILES)]
 
     def shallower(value):
-        turned = [jnp.zeros((SHOTS, 128), F32)] + [pltpu.roll(tile, 1, 1) for tile in value]
-        return [jnp.where(first_lane, turned[k], turned[k + 1]) for k in range(TILES)]
-
-    def stencil(above, here, below):
-        steep = [b + a for a, b in zip(above, below)]
-        slope = [b - a for a, b in zip(above, below)]
-        deep = [a + b for a, b in zip(deeper(here), shallower(here))]
-        cross = [a - b for a, b in zip(deeper(slope), shallower(slope))]
-        return steep, deep, cross
+        turned = [pltpu.roll(tile, 1, 1) for tile in value]
+        return [jnp.where(first_lane, turned[k - 1], turned[k]) for k in range(TILES)]
+
+    def mix(first, a, second, b, sign):
+        if sign > 0:
+            return [w * x + v * y for w, x, v, y in zip(first, a, second, b)]
+        return [w * x - v * y for w, x, v, y in zip(first, a, second, b)]
 
     def some_rows(moment, row, count):
         p_rows = [tiles(pbuf[moment, row + k]) for k in range(-1, count + 1)]
         q_rows = [tiles(qbuf[moment, row + k]) for k in range(-1, count + 1)]
         for k in range(count):
             at = row + k
-            cos_sq, sin_sq, twist, speed, speed_e, speed_d = (
+            (
+                cos_sq,
+                sin_sq,
+                speed,
+                speed_e,
+                speed_d,
+                cos_up,
+                sin_up,
+                twist_up,
+                cos_down,
+                sin_down,
+                twist_down,
+            ) = (
                 tiles(jnp.broadcast_to(coef[number, pl.ds(at + 4, 1)], (SHOTS, DEPTH)))
-                for number in range(6)
+                for number in (0, 1, 3, 4, 5, 6, 7, 8, 9, 10, 11)
             )
-            p_steep, p_deep, p_cross = stencil(p_rows[k], p_rows[k + 1], p_rows[k + 2])
-            q_steep, q_deep, q_cross = stencil(q_rows[k], q_rows[k + 1], q_rows[k + 2])
+            p_steep = [a + b for a, b in zip(p_rows[k], p_rows[k + 2])]
+            p_slope = [b - a for a, b in zip(p_rows[k], p_rows[k + 2])]
+            q_steep = [a + b for a, b in zip(q_rows[k], q_rows[k + 2])]
+            q_slope = [b - a for a, b in zip(q_rows[k], q_rows[k + 2])]
+            p_deeper = deeper(mix(sin_up, p_rows[k + 1], twist_up, p_slope, -1))
+            p_shallower = shallower(mix(sin_down, p_rows[k + 1], twist_down, p_slope, 1))
+            q_deeper = deeper(mix(cos_up, q_rows[k + 1], twist_up, q_slope, 1))
+            q_shallower = shallower(mix(cos_down, q_rows[k + 1], twist_down, q_slope, -1))
             p_old = tiles(pbuf[moment - 1, at])
             q_old = tiles(qbuf[moment - 1, at])
             for t in range(TILES):
                 p_two = p_rows[k + 1][t] + p_rows[k + 1][t]
                 q_two = q_rows[k + 1][t] + q_rows[k + 1][t]
-                across = (
-                    cos_sq[t] * p_steep[t] + sin_sq[t] * p_deep[t] - twist[t] * p_cross[t] - p_two
-                )
-                along = (
-                    sin_sq[t] * q_steep[t] + cos_sq[t] * q_deep[t] + twist[t] * q_cross[t] - q_two
-                )
+                across = (cos_sq[t] * p_steep[t] - p_two) + (p_deeper[t] + p_shallower[t])
+                along = (sin_sq[t] * q_steep[t] - q_two) + (q_deeper[t] + q_shallower[t])
                 push = speed[t] * along
                 lanes = pl.ds(128 * t, 128)
                 pbuf[moment + 1, at, :, lanes] = (p_two - p_old[t]) + (speed_e[t] * across + push)
@@ -237,13 +290,6 @@
         return lax.fori_loop(0, (ROWS - 2 * moment + 3) // 4, group, carry)
 
     lax.fori_loop(1, STEPS + 1, inner_step, 0)
-
-    cells = cells_ref[...]
-    target_x = cells >> 9
-    target_z = cells & (DEPTH - 1)
-    onehot[...] = (
-        lax.broadcasted_iota(jnp.int32, (DEPTH, DEPTH), 0) == target_z
-    ).astype(F32).astype(BF16)
 
     def picked(moment, first, count):
         rows = pbuf[moment + 1, pl.ds(first + HALO, count)].reshape(count * SHOTS, DEPTH)
@@ -263,15 +309,6 @@
         return carry
 
     lax.fori_loop(1, STEPS + 1, inner_samples, 0)
-
-    number = lax.broadcasted_iota(jnp.int32, (16, 128), 0)
-    frequency = jnp.zeros((16, 128), F32)
-    for k in range(16):
-        frequency = jnp.where(number == k, freq_ref[k], frequency)
-    tables = []
-    for moment in range(STEPS):
-        angle = frequency * (moment + 1.0)
-        tables.append(jnp.concatenate([jnp.cos(angle), -jnp.sin(angle)], axis=0))
 
     for side, there in ((0, has_left), (1, has_right)):
 
@@ -298,6 +335,10 @@
             qbuf[0, first + row] = both[SHOTS:]
         for k in range(6):
             coef[k, pl.ds(first + 4, 3)] = rim_in[side, pl.ds(4 * k, 3)]
+        up, down = shifted(rim_in[side, pl.ds(0, 16)])
+        for k in range(3):
+            coef[6 + k, pl.ds(first + 4, 3)] = up[4 * k : 4 * k + 3]
+            coef[9 + k, pl.ds(first + 4, 3)] = down[4 * k : 4 * k + 3]
 
     def outer_step(moment, carry):
         def group(side, carry):
@@ -336,7 +377,7 @@
             lanes = pl.ds(128 * t, 128)
             value = spec[s, :, lanes]
             for moment in range(STEPS):
-                value = value + tables[moment] * drawn[moment][:, 128 * t : 128 * (t + 1)]
+                value = value + table[moment] * drawn[moment][:, 128 * t : 128 * (t + 1)]
             spec[s, :, lanes] = value
             feats[core, pl.ds(s * 32, 32), lanes] = value.astype(BF16)
         return carry
@@ -473,16 +514,6 @@
         ring_copy(chip, lax.rem(chip + hop, CHIPS)).start()
     pass_copy(chip, core).start()
 
-    chosen = jnp.concatenate(
-        [
-            (lax.broadcasted_iota(jnp.int32, (512, PATCH), 0) == lists_ref[p, pl.ds(shot, 1)])
-            .astype(F32)
-            .astype(BF16)
-            for p in range(P_MAX)
-        ],
-        axis=1,
-    )
-
     for hop in NEAR_FIRST:
         place = lax.rem(chip + hop, CHIPS)
         ring_copy(place, place).wait_recv()
@@ -493,7 +524,7 @@
     strips = [None] * 4
     for which in range(2):
         grid = [gathered[which, k].astype(F32) for k in range(5)]
-        rows = [chosen[128 * (k % 4) : 128 * (k % 4 + 1)] for k in range(which, which + 4)]
+        rows = [chosen[pl.ds(128 * (k % 4), 128)] for k in range(which, which + 4)]
         for row, left, right in (
             (which, [0.5 * grid[0], grid[1], grid[2]], rows[0:3]),
             (which + 2, [0.5 * grid[3], grid[4]], rows[2:4]),
@@ -505,8 +536,8 @@
             )
     strip_high, strip_low = split(jnp.concatenate(strips, axis=0))
     root_high, root_low = split(jnp.broadcast_to(root * (1.0 / FULL), (8, DEPTH)))
-    chosen_root = jnp.dot(root_high, chosen, preferred_element_type=F32) + jnp.dot(
-        root_low, chosen, preferred_element_type=F32
+    chosen_root = jnp.dot(root_high, chosen[...], preferred_element_type=F32) + jnp.dot(
+        root_low, chosen[...], preferred_element_type=F32
     )
     for p in range(P_MAX):
         lanes = slice(PATCH * p, PATCH * (p + 1))
@@ -584,15 +615,18 @@
             pltpu.VMEM((SHOTS, 32, DEPTH), F32),
             pltpu.VMEM((P_MAX, PATCH, PATCH), F32),
         ),
-        in_specs=[smem, smem] + [vmem] * 6 + [whole] * 5,
+        in_specs=[smem, smem] + [whole] * 4 + [vmem] * 2 + [whole] * 5,
         out_specs=(vmem,) * 4,
         scratch_shapes=[
-            pltpu.VMEM((6, ROWS + 16, DEPTH), F32),
+            pltpu.VMEM((4, ROWS, DEPTH), F32),
+            pltpu.VMEM((12, ROWS + 16, DEPTH), F32),
             pltpu.VMEM((2, 7, 16, DEPTH), BF16),
             pltpu.VMEM((2, 7, 16, DEPTH), BF16),
             pltpu.VMEM((2, 24, DEPTH), F32),
             pltpu.VMEM((2, 24, DEPTH), F32),
             pltpu.VMEM((DEPTH, DEPTH), BF16),
+            pltpu.VMEM((512, P_MAX * PATCH), BF16),
+            pltpu.VMEM((STEPS, 32, 128), F32),
             pltpu.VMEM((STEPS, SHOTS, DEPTH), F32),
             pltpu.VMEM((2, SHOTS * 32, DEPTH), BF16),
             pltpu.VMEM((CHIPS, 8, DEPTH), F32),
@@ -600,7 +634,7 @@
             pltpu.VMEM((5, 128, 128), jnp.int16),
             pltpu.VMEM((CHIPS, 5, CHUNK, 128), jnp.int16),
             pltpu.VMEM((2, 5, 128, 128), jnp.int16),
-            dma((5,)),
+            dma((6,)),
             dma((2, 2)),
             dma((2, 2)),
             dma,

time: 44.4 us -> 43.7 us (0.984)
  Pallas kernels: 42.9 us -> 42.2 us
    pallas_call x1, Pallas kernels: 41.7 us -> 40.9 us  [shards(): pl.pallas_call(functools.partial(kernel, bricks), out_shape=(history, his...]
where the time goes in v3:
time: 43.7 us; the launch traced here: 43.4 us
  Pallas kernels  42.2 us (97%)
  between operations  1.29 us (3%)
    pallas_call x1, Pallas kernels, shards(): pl.pallas_call(functools.partial(kernel, bricks), out_shape=(history, his...  40.9 us
    pallas_call x1, Pallas kernels, shards(): pl.pallas_call(deliver, out_shape=(field, field, field, jax.ShapeDtypeStr...  1.22 us

profile of v3, /device:TPU:7, one launch (start us, length us, event | category | flops | bytes accessed | tf_op | source)
XLA Modules:
  0.0 43.4 jit_solution(18432352672298561746)
XLA Ops:
  1.3 40.9 %shard_map.156 = (f32[6,40,8,512]{3,2,1,0:T(8,128)S(1)}, f32[6,40,8,512]{3,2,1,0:T(8,128)S(1)}, f32[8,32,512]{2,1,0:T(8,128)S(1)}, f32[3,128,128]{2,1,0:T(8,128)S(1)}) custom-call(f32[16]{0:T(128)} %freq_ref.1, s32[1,1]{1,0:T(1,128)S(6)} %copy.17.counts_ref, f32[32,512]{1,0:T(8,128)} %courant_in.1, f32[32,512]{1,0:T(8,128)} %epsilon_in.1, ...), custom_call_target="tpu_custom_call" | custom-call | tf_op jit(solution)/shard_map/pallas_call | solution.py:610
  42.2 1.2 %shard_map.157 = (f32[8,32,512]{2,1,0:T(8,128)}, f32[8,32,512]{2,1,0:T(8,128)}, f32[8,32,512]{2,1,0:T(8,128)}, f32[3,128,128]{2,1,0:T(8,128)}) custom-call(f32[6,40,8,512]{3,2,1,0:T(8,128)S(1)} %get-tuple-element.12.pbuf, f32[6,40,8,512]{3,2,1,0:T(8,128)S(1)} %get-tuple-element.13.qbuf, f32[8,32,512]{2,1,0:T(8,128)S(1)} %get-tuple-element.14.spec, ...), custom_call_target="tpu_custom_call" | custom-call | tf_op jit(solution)/shard_map/pallas_call | solution.py:670

commit v4 on v3

--- a/solution.py
+++ b/solution.py
@@ -17,6 +17,7 @@
 TILES = DEPTH // 128
 CHIPS = 8
 CHUNK = 128 // CHIPS
+RIM = (0, 2, 3, 4, 5)
 FULL = 178.0
 MESH = pl.DeviceIdType.MESH
 F32 = jnp.float32
@@ -33,14 +34,14 @@
 
 def kernel(
     bricks,
-    freq_ref,
-    counts_ref,
+    freq_in,
+    counts_in,
     courant_in,
     epsilon_in,
     delta_in,
     tilt_in,
-    cells_ref,
-    lists_ref,
+    cells_in,
+    lists_in,
     p_in,
     q_in,
     pp_in,
@@ -50,6 +51,10 @@
     qbuf,
     spec,
     gram_ref,
+    freq_ref,
+    counts_ref,
+    cells_ref,
+    lists_ref,
     model,
     coef,
     slab_out,
@@ -66,6 +71,8 @@
     part_out,
     part_in,
     gathered,
+    strips,
+    word,
     in_sem,
     halo_send,
     halo_recv,
@@ -88,13 +95,11 @@
     has_right = brick < bricks - 1
 
     barrier = pltpu.get_barrier_semaphore()
-    for other in range(1, 2 * CHIPS):
-        pl.semaphore_signal(
-            barrier,
-            inc=1,
-            device_id={"shot": lax.rem(shot + other, 2 * CHIPS)},
-            device_id_type=MESH,
-        )
+    mate = {"shot": 2 * chip + 1 - core}
+    chip_up = {"shot": 2 * lax.rem(chip + 1, CHIPS) + core}
+    chip_down = {"shot": 2 * lax.rem(chip + CHIPS - 1, CHIPS) + core}
+    for other in (mate, chip_up, chip_down):
+        pl.semaphore_signal(barrier, inc=1, device_id=other, device_id_type=MESH)
 
     @pl.when(has_left)
     def _():
@@ -126,29 +131,19 @@
         load.start()
     spectra_load = pltpu.make_async_copy(spectra_in, spec, in_sem.at[4])
     spectra_load.start()
-
-    cells = cells_ref[...]
-    target_x = cells >> 9
-    target_z = cells & (DEPTH - 1)
-    onehot[...] = (
-        lax.broadcasted_iota(jnp.int32, (DEPTH, DEPTH), 0) == target_z
-    ).astype(F32).astype(BF16)
-
-    for p in range(P_MAX):
-        chosen[:, pl.ds(PATCH * p, PATCH)] = (
-            (lax.broadcasted_iota(jnp.int32, (512, PATCH), 0) == lists_ref[p, pl.ds(shot, 1)])
-            .astype(F32)
-            .astype(BF16)
-        )
-
-    number = lax.broadcasted_iota(jnp.int32, (16, 128), 0)
-    frequency = jnp.zeros((16, 128), F32)
-    for k in range(16):
-        frequency = jnp.where(number == k, freq_ref[k], frequency)
-    for moment in range(STEPS):
-        angle = frequency * (moment + 1.0)
-        table[moment, pl.ds(0, 16)] = jnp.cos(angle)
-        table[moment, pl.ds(16, 16)] = -jnp.sin(angle)
+    small_loads = [
+        pltpu.make_async_copy(source, target, in_sem.at[6 + k])
+        for k, (source, target) in enumerate(
+            (
+                (freq_in, freq_ref),
+                (counts_in, counts_ref),
+                (cells_in, cells_ref),
+                (lists_in, lists_ref),
+            )
+        )
+    ]
+    for load in small_loads:
+        load.start()
 
     def shifted(value):
         lane = lax.broadcasted_iota(jnp.int32, value.shape, 1)
@@ -170,11 +165,10 @@
     coef[3, own] = courant
     coef[4, own] = courant * (1.0 + 2.0 * model[1])
     coef[5, own] = courant * (1.0 + 2.0 * model[2])
-    for number in range(6):
-        rim_out[0, pl.ds(4 * number, 3)] = coef[number, pl.ds(8, 3)]
-        rim_out[1, pl.ds(4 * number, 3)] = coef[number, pl.ds(8 + ROWS - 3, 3)]
-        rim_out[:, pl.ds(4 * number + 3, 1)] = jnp.zeros((2, 1, DEPTH), F32)
-
+    for side, first in ((0, 8), (1, 8 + ROWS - 3)):
+        rim_out[side] = jnp.concatenate(
+            [coef[k, pl.ds(first, 3)] for k in RIM] + [jnp.zeros((1, DEPTH), F32)], axis=0
+        ).astype(BF16)
     for load in loads:
         load.wait()
     for side in range(2):
@@ -190,8 +184,18 @@
             ).astype(BF16)
 
     pl.semaphore_wait(
-        barrier, 2 * CHIPS - 1 + has_left.astype(jnp.int32) + has_right.astype(jnp.int32)
+        barrier, 3 + has_left.astype(jnp.int32) + has_right.astype(jnp.int32)
     )
+
+    def spread(j):
+        pl.semaphore_signal(word.at[j, 0], inc=1, device_id=chip_up, device_id_type=MESH)
+        pl.semaphore_signal(word.at[j, 1], inc=1, device_id=chip_down, device_id_type=MESH)
+
+    def hear(j):
+        pl.semaphore_wait(word.at[j, 0], 1)
+        pl.semaphore_wait(word.at[j, 1], 1)
+
+    spread(0)
 
     def halo_copies(side):
         target = {"brick": brick - 1 if side == 0 else brick + 1}
@@ -220,6 +224,31 @@
         def _():
             for copy in halo_copies(side):
                 copy.start()
+
+    for load in small_loads:
+        load.wait()
+    cells = cells_ref[...]
+    target_x = cells >> 9
+    target_z = cells & (DEPTH - 1)
+    onehot[...] = (
+        lax.broadcasted_iota(jnp.int32, (DEPTH, DEPTH), 0) == target_z
+    ).astype(F32).astype(BF16)
+
+    for p in range(P_MAX):
+        chosen[:, pl.ds(PATCH * p, PATCH)] = (
+            (lax.broadcasted_iota(jnp.int32, (512, PATCH), 0) == lists_ref[p, pl.ds(shot, 1)])
+            .astype(F32)
+            .astype(BF16)
+        )
+
+    number = lax.broadcasted_iota(jnp.int32, (16, 128), 0)
+    frequency = jnp.zeros((16, 128), F32)
+    for k in range(16):
+        frequency = jnp.where(number == k, freq_ref[k], frequency)
+    for moment in range(STEPS):
+        angle = frequency * (moment + 1.0)
+        table[moment, pl.ds(0, 16)] = jnp.cos(angle)
+        table[moment, pl.ds(16, 16)] = -jnp.sin(angle)
 
     lane = lax.broadcasted_iota(jnp.int32, (SHOTS, 128), 1)
     first_lane = lane == 0
@@ -290,6 +319,8 @@
         return lax.fori_loop(0, (ROWS - 2 * moment + 3) // 4, group, carry)
 
     lax.fori_loop(1, STEPS + 1, inner_step, 0)
+    hear(0)
+    spread(1)
 
     def picked(moment, first, count):
         rows = pbuf[moment + 1, pl.ds(first + HALO, count)].reshape(count * SHOTS, DEPTH)
@@ -309,6 +340,8 @@
         return carry
 
     lax.fori_loop(1, STEPS + 1, inner_samples, 0)
+    hear(1)
+    spread(2)
 
     for side, there in ((0, has_left), (1, has_right)):
 
@@ -320,7 +353,7 @@
         @pl.when(jnp.logical_not(there))
         def _():
             slab_in[side] = jnp.zeros((7, 16, DEPTH), BF16)
-            rim_in[side] = jnp.zeros((24, DEPTH), F32)
+            rim_in[side] = jnp.zeros((16, DEPTH), BF16)
 
     for side in range(2):
         first = 0 if side == 0 else HALO + ROWS
@@ -333,12 +366,21 @@
             both = slab_in[side, 4 + row].astype(F32)
             pbuf[0, first + row] = both[:SHOTS]
             qbuf[0, first + row] = both[SHOTS:]
-        for k in range(6):
-            coef[k, pl.ds(first + 4, 3)] = rim_in[side, pl.ds(4 * k, 3)]
-        up, down = shifted(rim_in[side, pl.ds(0, 16)])
-        for k in range(3):
-            coef[6 + k, pl.ds(first + 4, 3)] = up[4 * k : 4 * k + 3]
-            coef[9 + k, pl.ds(first + 4, 3)] = down[4 * k : 4 * k + 3]
+        rim = rim_in[side].astype(F32)
+        for k, number in enumerate(RIM):
+            coef[number, pl.ds(first + 4, 3)] = rim[3 * k : 3 * k + 3]
+        coef[1, pl.ds(first + 4, 3)] = 1.0 - rim[:3]
+        turns_up, turns_down = shifted(rim[:8])
+        rest_up, rest_down = shifted(1.0 - rim[:8])
+        for number, value, start in (
+            (6, turns_up, 0),
+            (7, rest_up, 0),
+            (8, turns_up, 3),
+            (9, turns_down, 0),
+            (10, rest_down, 0),
+            (11, turns_down, 3),
+        ):
+            coef[number, pl.ds(first + 4, 3)] = value[start : start + 3]
 
     def outer_step(moment, carry):
         def group(side, carry):
@@ -384,7 +426,6 @@
 
     lax.fori_loop(0, SHOTS, transform, 0)
 
-    mate = {"shot": 2 * chip + 1 - core}
     feat_copy = pltpu.make_async_remote_copy(
         src_ref=feats.at[core],
         dst_ref=feats.at[core],
@@ -411,6 +452,7 @@
             device_id_type=MESH,
         )
 
+    hear(2)
     for hop in FAR_FIRST:
         energy_copy(lax.rem(chip + hop, CHIPS), chip).start()
 
@@ -518,23 +560,30 @@
         place = lax.rem(chip + hop, CHIPS)
         ring_copy(place, place).wait_recv()
         pass_copy(place, core).start()
-    for hop in (0,) + NEAR_FIRST:
-        pass_copy(lax.rem(chip + hop, CHIPS), 1 - core).wait_recv()
-
-    strips = [None] * 4
-    for which in range(2):
+    def strips_of(which):
         grid = [gathered[which, k].astype(F32) for k in range(5)]
-        rows = [chosen[pl.ds(128 * (k % 4), 128)] for k in range(which, which + 4)]
+
+        def picks(first, count):
+            return [
+                chosen[pl.ds(pl.multiple_of(lax.rem(which + k, 4) * 128, 128), 128)]
+                for k in range(first, first + count)
+            ]
+
         for row, left, right in (
-            (which, [0.5 * grid[0], grid[1], grid[2]], rows[0:3]),
-            (which + 2, [0.5 * grid[3], grid[4]], rows[2:4]),
+            (0, [0.5 * grid[0], grid[1], grid[2]], picks(0, 3)),
+            (2, [0.5 * grid[3], grid[4]], picks(2, 2)),
         ):
             high, low = split(jnp.concatenate(left, axis=1))
             right = jnp.concatenate(right, axis=0)
-            strips[row] = jnp.dot(high, right, preferred_element_type=F32) + jnp.dot(
+            strips[which + row] = jnp.dot(high, right, preferred_element_type=F32) + jnp.dot(
                 low, right, preferred_element_type=F32
             )
-    strip_high, strip_low = split(jnp.concatenate(strips, axis=0))
+
+    strips_of(core)
+    for hop in (0,) + NEAR_FIRST:
+        pass_copy(lax.rem(chip + hop, CHIPS), 1 - core).wait_recv()
+    strips_of(1 - core)
+    strip_high, strip_low = split(strips[...].reshape(512, P_MAX * PATCH))
     root_high, root_low = split(jnp.broadcast_to(root * (1.0 / FULL), (8, DEPTH)))
     chosen_root = jnp.dot(root_high, chosen[...], preferred_element_type=F32) + jnp.dot(
         root_low, chosen[...], preferred_element_type=F32
@@ -603,7 +652,6 @@
     patch_counts,
 ):
     vmem = pl.BlockSpec(memory_space=pltpu.VMEM)
-    smem = pl.BlockSpec(memory_space=pltpu.SMEM)
     whole = pl.BlockSpec(memory_space=pltpu.HBM)
     history = pltpu.VMEM((STEPS + 2, ROWS + 2 * HALO, SHOTS, DEPTH), F32)
     dma = pltpu.SemaphoreType.DMA
@@ -615,15 +663,19 @@
             pltpu.VMEM((SHOTS, 32, DEPTH), F32),
             pltpu.VMEM((P_MAX, PATCH, PATCH), F32),
         ),
-        in_specs=[smem, smem] + [whole] * 4 + [vmem] * 2 + [whole] * 5,
+        in_specs=[whole] * 13,
         out_specs=(vmem,) * 4,
         scratch_shapes=[
+            pltpu.SMEM((16,), F32),
+            pltpu.SMEM((1, 1), jnp.int32),
+            pltpu.VMEM((1, DEPTH), jnp.int32),
+            pltpu.VMEM((P_MAX, 2 * CHIPS, PATCH), jnp.int32),
             pltpu.VMEM((4, ROWS, DEPTH), F32),
             pltpu.VMEM((12, ROWS + 16, DEPTH), F32),
             pltpu.VMEM((2, 7, 16, DEPTH), BF16),
             pltpu.VMEM((2, 7, 16, DEPTH), BF16),
-            pltpu.VMEM((2, 24, DEPTH), F32),
-            pltpu.VMEM((2, 24, DEPTH), F32),
+            pltpu.VMEM((2, 16, DEPTH), BF16),
+            pltpu.VMEM((2, 16, DEPTH), BF16),
             pltpu.VMEM((DEPTH, DEPTH), BF16),
             pltpu.VMEM((512, P_MAX * PATCH), BF16),
             pltpu.VMEM((STEPS, 32, 128), F32),
@@ -634,7 +686,9 @@
             pltpu.VMEM((5, 128, 128), jnp.int16),
             pltpu.VMEM((CHIPS, 5, CHUNK, 128), jnp.int16),
             pltpu.VMEM((2, 5, 128, 128), jnp.int16),
-            dma((6,)),
+            pltpu.VMEM((4, 128, P_MAX * PATCH), F32),
+            pltpu.SemaphoreType.REGULAR((3, 2)),
+            dma((10,)),
             dma((2, 2)),
             dma((2, 2)),
             dma,

time: 43.7 us -> 40.9 us (0.936)
  Pallas kernels: 42.2 us -> 39.4 us
    pallas_call x1, Pallas kernels: 40.9 us -> 38.2 us  [shards(): pl.pallas_call(functools.partial(kernel, bricks), out_shape=(history, his...]
where the time goes in v4:
time: 40.9 us; the launch traced here: 40.7 us
  Pallas kernels  39.4 us (96%)
  between operations  1.29 us (3%)
    pallas_call x1, Pallas kernels, shards(): pl.pallas_call(functools.partial(kernel, bricks), out_shape=(history, his...  38.2 us
    pallas_call x1, Pallas kernels, shards(): pl.pallas_call(deliver, out_shape=(field, field, field, jax.ShapeDtypeStr...  1.22 us

profile of v4, /device:TPU:7, one launch (start us, length us, event | category | flops | bytes accessed | tf_op | source)
XLA Modules:
  0.0 40.7 jit_solution(5836715218457421308)
XLA Ops:
  1.3 38.2 %shard_map.156 = (f32[6,40,8,512]{3,2,1,0:T(8,128)S(1)}, f32[6,40,8,512]{3,2,1,0:T(8,128)S(1)}, f32[8,32,512]{2,1,0:T(8,128)S(1)}, f32[3,128,128]{2,1,0:T(8,128)S(1)}) custom-call(f32[16]{0:T(128)} %freq_in.1, s32[1,1]{1,0:T(1,128)S(6)} %copy.17.counts_in, f32[32,512]{1,0:T(8,128)} %courant_in.1, f32[32,512]{1,0:T(8,128)} %epsilon_in.1, f32[32,512]{1,0:T(8,128)} %delta_in.1, ...), custom_call_target="tpu_custom_call" | custom-call | tf_op jit(solution)/shard_map/pallas_call | solution.py:658
  39.5 1.2 %shard_map.157 = (f32[8,32,512]{2,1,0:T(8,128)}, f32[8,32,512]{2,1,0:T(8,128)}, f32[8,32,512]{2,1,0:T(8,128)}, f32[3,128,128]{2,1,0:T(8,128)}) custom-call(f32[6,40,8,512]{3,2,1,0:T(8,128)S(1)} %get-tuple-element.12.pbuf, f32[6,40,8,512]{3,2,1,0:T(8,128)S(1)} %get-tuple-element.13.qbuf, f32[8,32,512]{2,1,0:T(8,128)S(1)} %get-tuple-element.14.spec, ...), custom_call_target="tpu_custom_call" | custom-call | tf_op jit(solution)/shard_map/pallas_call | solution.py:724

commit v5 on v4

--- a/solution.py
+++ b/solution.py
@@ -171,85 +171,6 @@
         ).astype(BF16)
     for load in loads:
         load.wait()
-    for side in range(2):
-        first = HALO if side == 0 else HALO + ROWS - 4
-        for row in range(4):
-            slab_out[side, row] = jnp.concatenate(
-                [pbuf[1, first + row], qbuf[1, first + row]], axis=0
-            ).astype(BF16)
-        first = HALO if side == 0 else HALO + ROWS - 3
-        for row in range(3):
-            slab_out[side, 4 + row] = jnp.concatenate(
-                [pbuf[0, first + row], qbuf[0, first + row]], axis=0
-            ).astype(BF16)
-
-    pl.semaphore_wait(
-        barrier, 3 + has_left.astype(jnp.int32) + has_right.astype(jnp.int32)
-    )
-
-    def spread(j):
-        pl.semaphore_signal(word.at[j, 0], inc=1, device_id=chip_up, device_id_type=MESH)
-        pl.semaphore_signal(word.at[j, 1], inc=1, device_id=chip_down, device_id_type=MESH)
-
-    def hear(j):
-        pl.semaphore_wait(word.at[j, 0], 1)
-        pl.semaphore_wait(word.at[j, 1], 1)
-
-    spread(0)
-
-    def halo_copies(side):
-        target = {"brick": brick - 1 if side == 0 else brick + 1}
-        return [
-            pltpu.make_async_remote_copy(
-                src_ref=slab_out.at[side],
-                dst_ref=slab_in.at[1 - side],
-                send_sem=halo_send.at[side, 0],
-                recv_sem=halo_recv.at[1 - side, 0],
-                device_id=target,
-                device_id_type=MESH,
-            ),
-            pltpu.make_async_remote_copy(
-                src_ref=rim_out.at[side],
-                dst_ref=rim_in.at[1 - side],
-                send_sem=halo_send.at[side, 1],
-                recv_sem=halo_recv.at[1 - side, 1],
-                device_id=target,
-                device_id_type=MESH,
-            ),
-        ]
-
-    for side, there in ((0, has_left), (1, has_right)):
-
-        @pl.when(there)
-        def _():
-            for copy in halo_copies(side):
-                copy.start()
-
-    for load in small_loads:
-        load.wait()
-    cells = cells_ref[...]
-    target_x = cells >> 9
-    target_z = cells & (DEPTH - 1)
-    onehot[...] = (
-        lax.broadcasted_iota(jnp.int32, (DEPTH, DEPTH), 0) == target_z
-    ).astype(F32).astype(BF16)
-
-    for p in range(P_MAX):
-        chosen[:, pl.ds(PATCH * p, PATCH)] = (
-            (lax.broadcasted_iota(jnp.int32, (512, PATCH), 0) == lists_ref[p, pl.ds(shot, 1)])
-            .astype(F32)
-            .astype(BF16)
-        )
-
-    number = lax.broadcasted_iota(jnp.int32, (16, 128), 0)
-    frequency = jnp.zeros((16, 128), F32)
-    for k in range(16):
-        frequency = jnp.where(number == k, freq_ref[k], frequency)
-    for moment in range(STEPS):
-        angle = frequency * (moment + 1.0)
-        table[moment, pl.ds(0, 16)] = jnp.cos(angle)
-        table[moment, pl.ds(16, 16)] = -jnp.sin(angle)
-
     lane = lax.broadcasted_iota(jnp.int32, (SHOTS, 128), 1)
     first_lane = lane == 0
     last_lane = lane == 127
@@ -311,6 +232,83 @@
                 pbuf[moment + 1, at, :, lanes] = (p_two - p_old[t]) + (speed_e[t] * across + push)
                 qbuf[moment + 1, at, :, lanes] = (q_two - q_old[t]) + (speed_d[t] * across + push)
 
+    some_rows(1, HALO + 1, 2)
+    some_rows(1, HALO + ROWS - 3, 2)
+
+    sent = (((1, 0), (1, 1), (0, 0), (2, 1), (2, 2)), ((1, 31), (1, 30), (0, 31), (2, 30), (2, 29)))
+    for side in range(2):
+        for k, (time, x) in enumerate(sent[side]):
+            slab_out[side, k] = jnp.concatenate(
+                [pbuf[time, HALO + x], qbuf[time, HALO + x]], axis=0
+            ).astype(BF16)
+
+    pl.semaphore_wait(
+        barrier, 3 + has_left.astype(jnp.int32) + has_right.astype(jnp.int32)
+    )
+
+    def spread(j):
+        pl.semaphore_signal(word.at[j, 0], inc=1, device_id=chip_up, device_id_type=MESH)
+        pl.semaphore_signal(word.at[j, 1], inc=1, device_id=chip_down, device_id_type=MESH)
+
+    def hear(j):
+        pl.semaphore_wait(word.at[j, 0], 1)
+        pl.semaphore_wait(word.at[j, 1], 1)
+
+    spread(0)
+
+    def halo_copies(side):
+        target = {"brick": brick - 1 if side == 0 else brick + 1}
+        return [
+            pltpu.make_async_remote_copy(
+                src_ref=slab_out.at[side],
+                dst_ref=slab_in.at[1 - side],
+                send_sem=halo_send.at[side, 0],
+                recv_sem=halo_recv.at[1 - side, 0],
+                device_id=target,
+                device_id_type=MESH,
+            ),
+            pltpu.make_async_remote_copy(
+                src_ref=rim_out.at[side],
+                dst_ref=rim_in.at[1 - side],
+                send_sem=halo_send.at[side, 1],
+                recv_sem=halo_recv.at[1 - side, 1],
+                device_id=target,
+                device_id_type=MESH,
+            ),
+        ]
+
+    for side, there in ((0, has_left), (1, has_right)):
+
+        @pl.when(there)
+        def _():
+            for copy in halo_copies(side):
+                copy.start()
+
+    for load in small_loads:
+        load.wait()
+    cells = cells_ref[...]
+    target_x = cells >> 9
+    target_z = cells & (DEPTH - 1)
+    onehot[...] = (
+        lax.broadcasted_iota(jnp.int32, (DEPTH, DEPTH), 0) == target_z
+    ).astype(F32).astype(BF16)
+
+    for p in range(P_MAX):
+        chosen[:, pl.ds(PATCH * p, PATCH)] = (
+            (lax.broadcasted_iota(jnp.int32, (512, PATCH), 0) == lists_ref[p, pl.ds(shot, 1)])
+            .astype(F32)
+            .astype(BF16)
+        )
+
+    number = lax.broadcasted_iota(jnp.int32, (16, 128), 0)
+    frequency = jnp.zeros((16, 128), F32)
+    for k in range(16):
+        frequency = jnp.where(number == k, freq_ref[k], frequency)
+    for moment in range(STEPS):
+        angle = frequency * (moment + 1.0)
+        table[moment, pl.ds(0, 16)] = jnp.cos(angle)
+        table[moment, pl.ds(16, 16)] = -jnp.sin(angle)
+
     def inner_step(moment, carry):
         def group(number, carry):
             some_rows(moment, moment + HALO + 4 * number, 4)
@@ -352,20 +350,16 @@
 
         @pl.when(jnp.logical_not(there))
         def _():
-            slab_in[side] = jnp.zeros((7, 16, DEPTH), BF16)
+            slab_in[side] = jnp.zeros((5, 16, DEPTH), BF16)
             rim_in[side] = jnp.zeros((16, DEPTH), BF16)
 
     for side in range(2):
-        first = 0 if side == 0 else HALO + ROWS
-        for row in range(4):
-            both = slab_in[side, row].astype(F32)
-            pbuf[1, first + row] = both[:SHOTS]
-            qbuf[1, first + row] = both[SHOTS:]
+        away = -ROWS if side == 0 else ROWS
+        for k, (time, x) in enumerate(sent[1 - side]):
+            both = slab_in[side, k].astype(F32)
+            pbuf[time, HALO + x + away] = both[:SHOTS]
+            qbuf[time, HALO + x + away] = both[SHOTS:]
         first = 1 if side == 0 else HALO + ROWS
-        for row in range(3):
-            both = slab_in[side, 4 + row].astype(F32)
-            pbuf[0, first + row] = both[:SHOTS]
-            qbuf[0, first + row] = both[SHOTS:]
         rim = rim_in[side].astype(F32)
         for k, number in enumerate(RIM):
             coef[number, pl.ds(first + 4, 3)] = rim[3 * k : 3 * k + 3]
@@ -389,7 +383,9 @@
 
         return lax.fori_loop(0, 2, group, carry)
 
-    lax.fori_loop(1, STEPS + 1, outer_step, 0)
+    some_rows(1, HALO - 1, 2)
+    some_rows(1, HALO + ROWS - 1, 2)
+    lax.fori_loop(2, STEPS + 1, outer_step, 0)
 
     edges = jnp.concatenate(
         [
@@ -413,6 +409,17 @@
 
     spectra_load.wait()
 
+    def feat_copy(s):
+        rows = pl.ds(pl.multiple_of(s * 32, 32), 32)
+        return pltpu.make_async_remote_copy(
+            src_ref=feats.at[core, rows],
+            dst_ref=feats.at[core, rows],
+            send_sem=feat_send.at[s],
+            recv_sem=feat_recv.at[s],
+            device_id=mate,
+            device_id_type=MESH,
+        )
+
     def transform(s, carry):
         drawn = [samples[moment, pl.ds(s, 1)] for moment in range(STEPS)]
         for t in range(TILES):
@@ -422,25 +429,42 @@
                 value = value + table[moment] * drawn[moment][:, 128 * t : 128 * (t + 1)]
             spec[s, :, lanes] = value
             feats[core, pl.ds(s * 32, 32), lanes] = value.astype(BF16)
+        feat_copy(s).start()
         return carry
 
     lax.fori_loop(0, SHOTS, transform, 0)
 
-    feat_copy = pltpu.make_async_remote_copy(
-        src_ref=feats.at[core],
-        dst_ref=feats.at[core],
-        send_sem=feat_send,
-        recv_sem=feat_recv,
-        device_id=mate,
-        device_id_type=MESH,
-    )
-    feat_copy.start()
-    feat_copy.wait_recv()
-
-    both = feats[...].reshape(2 * SHOTS * 32, DEPTH)
-    energy[chip] = jnp.dot(
-        jnp.ones((8, 2 * SHOTS * 32), BF16), both * both, preferred_element_type=F32
-    )
+    def energy_of(which):
+        rows = feats[which]
+        return jnp.dot(
+            jnp.ones((8, SHOTS * 32), BF16), rows * rows, preferred_element_type=F32
+        )
+
+    pairs = ((0, 0), (0, 1), (0, 2), (2, 2), (2, 3))
+
+    def products_of(which):
+        blocks = [
+            feats[which, :, pl.ds(pl.multiple_of(lax.rem(core + k, 4) * 128, 128), 128)]
+            for k in range(4)
+        ]
+        found = []
+        for left, right in ((0, (0, 1, 2)), (2, (2, 3))):
+            product = lax.dot_general(
+                blocks[left],
+                jnp.concatenate([blocks[k] for k in right], axis=1),
+                (((0,), (0,)), ((), ())),
+                preferred_element_type=F32,
+            )
+            found += [product[:, 128 * k : 128 * (k + 1)] for k in range(len(right))]
+        return found
+
+    own_energy = energy_of(core)
+    for number, product in enumerate(products_of(core)):
+        half[number] = product
+    for s in range(SHOTS):
+        feat_copy(s).wait_recv()
+
+    energy[chip] = own_energy + energy_of(1 - core)
 
     def energy_copy(place, owner):
         return pltpu.make_async_remote_copy(
@@ -465,11 +489,6 @@
         straight = [row[:, 128 * k : 128 * (k + 1)] for k in range(4)]
         return [jnp.where(core == 0, straight[k], straight[(k + 1) % 4]) for k in range(4)]
 
-    pairs = ((0, 0), (0, 1), (0, 2), (2, 2), (2, 3))
-    blocks = [
-        feats[:, :, pl.ds(pl.multiple_of(lax.rem(core + k, 4) * 128, 128), 128)].reshape(512, 128)
-        for k in range(4)
-    ]
     row_number = lax.broadcasted_iota(jnp.int32, (128, 128), 0)
     lane_number = lax.broadcasted_iota(jnp.int32, (128, 128), 1)
 
@@ -479,19 +498,13 @@
 
     inverses = in_order(units(chip)[1])
     columns = {k: upright(inverses[k] * FULL, 0, 128) for k in (0, 2)}
-    number = 0
-    for left, right in ((0, (0, 1, 2)), (2, (2, 3))):
-        product = lax.dot_general(
-            blocks[left],
-            jnp.concatenate([blocks[k] for k in right], axis=1),
-            (((0,), (0,)), ((), ())),
-            preferred_element_type=F32,
-        )
-        for k, block in enumerate(right):
-            value = product[:, 128 * k : 128 * (k + 1)]
-            half[number] = value
-            part_out[number] = jnp.round(value * columns[left] * (inverses[block] * FULL)).astype(jnp.int16)
-            number += 1
+    for number, product in enumerate(products_of(1 - core)):
+        left, right = pairs[number]
+        value = half[number] + product
+        half[number] = value
+        part_out[number] = jnp.round(value * columns[left] * (inverses[right] * FULL)).astype(
+            jnp.int16
+        )
 
     def rows_of(place):
         return pl.ds(pl.multiple_of(place * CHUNK, CHUNK), CHUNK)
@@ -607,7 +620,8 @@
             for copy in halo_copies(side):
                 copy.wait_send()
 
-    feat_copy.wait_send()
+    for s in range(SHOTS):
+        feat_copy(s).wait_send()
     for hop in FAR_FIRST:
         place = lax.rem(chip + hop, CHIPS)
         energy_copy(place, chip).wait_send()
@@ -672,8 +686,8 @@
             pltpu.VMEM((P_MAX, 2 * CHIPS, PATCH), jnp.int32),
             pltpu.VMEM((4, ROWS, DEPTH), F32),
             pltpu.VMEM((12, ROWS + 16, DEPTH), F32),
-            pltpu.VMEM((2, 7, 16, DEPTH), BF16),
-            pltpu.VMEM((2, 7, 16, DEPTH), BF16),
+            pltpu.VMEM((2, 5, 16, DEPTH), BF16),
+            pltpu.VMEM((2, 5, 16, DEPTH), BF16),
             pltpu.VMEM((2, 16, DEPTH), BF16),
             pltpu.VMEM((2, 16, DEPTH), BF16),
             pltpu.VMEM((DEPTH, DEPTH), BF16),
@@ -691,8 +705,8 @@
             dma((10,)),
             dma((2, 2)),
             dma((2, 2)),
-            dma,
-            dma,
+            dma((SHOTS,)),
+            dma((SHOTS,)),
             dma((CHIPS,)),
             dma((CHIPS,)),
             dma((CHIPS,)),

time: 40.9 us -> 40.6 us (level)
  no operation moved by 1% of the time
where the time goes in v5:
time: 40.6 us; the launch traced here: 40.5 us
  Pallas kernels  39.2 us (97%)
  between operations  1.29 us (3%)
    pallas_call x1, Pallas kernels, shards(): pl.pallas_call(functools.partial(kernel, bricks), out_shape=(history, his...  38 us
    pallas_call x1, Pallas kernels, shards(): pl.pallas_call(deliver, out_shape=(field, field, field, jax.ShapeDtypeStr...  1.22 us

profile of v5, /device:TPU:7, one launch (start us, length us, event | category | flops | bytes accessed | tf_op | source)
XLA Modules:
  0.0 40.5 jit_solution(5076861378242729394)
XLA Ops:
  1.3 38.0 %shard_map.156 = (f32[6,40,8,512]{3,2,1,0:T(8,128)S(1)}, f32[6,40,8,512]{3,2,1,0:T(8,128)S(1)}, f32[8,32,512]{2,1,0:T(8,128)S(1)}, f32[3,128,128]{2,1,0:T(8,128)S(1)}) custom-call(f32[16]{0:T(128)} %freq_in.1, s32[1,1]{1,0:T(1,128)S(6)} %copy.17.counts_in, f32[32,512]{1,0:T(8,128)} %courant_in.1, f32[32,512]{1,0:T(8,128)} %epsilon_in.1, f32[32,512]{1,0:T(8,128)} %delta_in.1, ...), custom_call_target="tpu_custom_call" | custom-call | tf_op jit(solution)/shard_map/pallas_call | solution.py:672
  39.2 1.2 %shard_map.157 = (f32[8,32,512]{2,1,0:T(8,128)}, f32[8,32,512]{2,1,0:T(8,128)}, f32[8,32,512]{2,1,0:T(8,128)}, f32[3,128,128]{2,1,0:T(8,128)}) custom-call(f32[6,40,8,512]{3,2,1,0:T(8,128)S(1)} %get-tuple-element.12.pbuf, f32[6,40,8,512]{3,2,1,0:T(8,128)S(1)} %get-tuple-element.13.qbuf, f32[8,32,512]{2,1,0:T(8,128)S(1)} %get-tuple-element.14.spec, ...), custom_call_target="tpu_custom_call" | custom-call | tf_op jit(solution)/shard_map/pallas_call | solution.py:738

commit v6 on v5

--- a/solution.py
+++ b/solution.py
@@ -377,11 +377,9 @@
             coef[number, pl.ds(first + 4, 3)] = value[start : start + 3]
 
     def outer_step(moment, carry):
-        def group(side, carry):
-            some_rows(moment, jnp.where(side == 0, moment, HALO + ROWS - moment), 4)
-            return carry
-
-        return lax.fori_loop(0, 2, group, carry)
+        some_rows(moment, moment, 4)
+        some_rows(moment, HALO + ROWS - moment, 4)
+        return carry
 
     some_rows(1, HALO - 1, 2)
     some_rows(1, HALO + ROWS - 1, 2)

time: 40.6 us -> 40.6 us (level)
  no operation moved by 1% of the time
where the time goes in v6:
time: 40.6 us; the launch traced here: 40.5 us
  Pallas kernels  39.2 us (97%)
  between operations  1.29 us (3%)
    pallas_call x1, Pallas kernels, shards(): pl.pallas_call(functools.partial(kernel, bricks), out_shape=(history, his...  37.9 us
    pallas_call x1, Pallas kernels, shards(): pl.pallas_call(deliver, out_shape=(field, field, field, jax.ShapeDtypeStr...  1.22 us

profile of v6, /device:TPU:7, one launch (start us, length us, event | category | flops | bytes accessed | tf_op | source)
XLA Modules:
  0.0 40.5 jit_solution(645856746934795128)
XLA Ops:
  1.3 37.9 %shard_map.156 = (f32[6,40,8,512]{3,2,1,0:T(8,128)S(1)}, f32[6,40,8,512]{3,2,1,0:T(8,128)S(1)}, f32[8,32,512]{2,1,0:T(8,128)S(1)}, f32[3,128,128]{2,1,0:T(8,128)S(1)}) custom-call(f32[16]{0:T(128)} %freq_in.1, s32[1,1]{1,0:T(1,128)S(6)} %copy.17.counts_in, f32[32,512]{1,0:T(8,128)} %courant_in.1, f32[32,512]{1,0:T(8,128)} %epsilon_in.1, f32[32,512]{1,0:T(8,128)} %delta_in.1, ...), custom_call_target="tpu_custom_call" | custom-call | tf_op jit(solution)/shard_map/pallas_call | solution.py:670
  39.2 1.2 %shard_map.157 = (f32[8,32,512]{2,1,0:T(8,128)}, f32[8,32,512]{2,1,0:T(8,128)}, f32[8,32,512]{2,1,0:T(8,128)}, f32[3,128,128]{2,1,0:T(8,128)}) custom-call(f32[6,40,8,512]{3,2,1,0:T(8,128)S(1)} %get-tuple-element.12.pbuf, f32[6,40,8,512]{3,2,1,0:T(8,128)S(1)} %get-tuple-element.13.qbuf, f32[8,32,512]{2,1,0:T(8,128)S(1)} %get-tuple-element.14.spec, ...), custom_call_target="tpu_custom_call" | custom-call | tf_op jit(solution)/shard_map/pallas_call | solution.py:736
